TPU v7x, 32 devices: a whole 2x2x4 slice. The times are simulated.
32 devices in a mesh: tab: 8 (over z, x), blk: 4 (over y, core).
Axes of the slice: x: 2, y: 2, z: 4, core: 2. Of those that a mesh axis runs over, the one named last changes fastest.
Arguments:
- tables: bfloat16 [64, 512, 768], P('tab', 'blk'), may hold values from -6 to 6
- lengths: int32 [64], P('tab'), may hold values from 60 to 512, as said below
- cotangent: bfloat16 [64, 512, 768], P('tab', 'blk'), may hold values from -6 to 6
- step_count: int32 [1], replicated, may hold values from 2 to 20
- w_qkv: float32 [768, 2304], P('tab'), may hold values from -0.21875 to 0.21875
- w_out: float32 [768, 768], P('tab'), may hold values from -3.5 to 3.5
- w_up: float32 [768, 3072], P('tab'), may hold values from -0.21875 to 0.21875
- w_down: float32 [3072, 768], P('tab'), may hold values from -0.109375 to 0.109375
- vectors: float32 [768, 12], P('tab')
- first_qkv: float32 [768, 2304], P('tab'), may hold values from -128 to 128
- first_out: float32 [768, 768], P('tab'), may hold values from -12 to 12
- first_up: float32 [768, 3072], P('tab'), may hold values from -80 to 80
- first_down: float32 [3072, 768], P('tab'), may hold values from -64 to 64
- first_vec: float32 [768, 12], P('tab'), may hold values from -128 to 128
- second_qkv: float32 [768, 2304], P('tab'), may hold values from 16.384 to 262.144
- second_out: float32 [768, 768], P('tab'), may hold values from 0.16384 to 2.62144
- second_up: float32 [768, 3072], P('tab'), may hold values from 8.192 to 131.072
- second_down: float32 [3072, 768], P('tab'), may hold values from 5.89824 to 95.0272
- second_vec: float32 [768, 12], P('tab'), may hold values from 16.384 to 262.144
Outputs:
- output: bfloat16 [64, 512, 768], P('tab', 'blk')
- grad_input: float32 [64, 512, 768], P('tab', 'blk')
- moment_qkv: float32 [768, 2304], P('tab')
- square_qkv: float32 [768, 2304], P('tab')
- master_qkv: float32 [768, 2304], P('tab')
- copy_qkv: bfloat16 [768, 2304], P('tab')
- moment_out: float32 [768, 768], P('tab')
- square_out: float32 [768, 768], P('tab')
- master_out: float32 [768, 768], P('tab')
- copy_out: bfloat16 [768, 768], P('tab')
- moment_up: float32 [768, 3072], P('tab')
- square_up: float32 [768, 3072], P('tab')
- master_up: float32 [768, 3072], P('tab')
- copy_up: bfloat16 [768, 3072], P('tab')
- moment_down: float32 [3072, 768], P('tab')
- square_down: float32 [3072, 768], P('tab')
- master_down: float32 [3072, 768], P('tab')
- copy_down: bfloat16 [3072, 768], P('tab')
- moment_vec: float32 [768, 12], P('tab')
- square_vec: float32 [768, 12], P('tab')
- master_vec: float32 [768, 12], P('tab')
- copy_vec: bfloat16 [768, 12], P('tab')
Inputs may be any that keep to these rules, and one draw needn't show every extreme that they name: `lengths`: positions from a table's length on are padding; some table has exactly 512 live tokens.
All inputs are finite; a program needn't handle non-finite values.
Results may differ from a plain program's by a relative error of at most 0.018.
Values may be sent and summed in bfloat16 or wider, within the bound.
A program may use at most 256 MiB of HBM per device.

v0:
```python
from functools import partial

import jax
import jax.numpy as jnp
from jax import lax
from jax.sharding import PartitionSpec as P

D = 768
H = 12
HD = 64
LEN = 512


EPS = 1e-06
NEGATIVE = -1e30
BETA_ONE = 0.9
BETA_TWO = 0.999
ADAM_EPS = 1e-08
DECAY = 0.01
RATES = (1.0, 15.0, 1.0, 0.5, 5.0)


def layer_norm(hidden, gain_vec, shift_vec):
    row_mean = jnp.mean(hidden, axis=-1, keepdims=True)
    centred = hidden - row_mean
    variance = jnp.mean(centred * centred, axis=-1, keepdims=True)
    return centred * lax.rsqrt(variance + EPS) * gain_vec + shift_vec


def inner(left, right):
    return lax.dot_general(
        left, right, (((0,), (0,)), ((), ())), preferred_element_type=jnp.float32
    )


def back_mul(left, right):
    return lax.dot_general(
        left, right, (((1,), (1,)), ((), ())), preferred_element_type=jnp.float32
    )


def adam(master, gradient, first_moment, second_moment, rate_now, step_float):
    moment_new = BETA_ONE * first_moment + (1.0 - BETA_ONE) * gradient
    square_new = BETA_TWO * second_moment + (1.0 - BETA_TWO) * gradient * gradient
    fix_one = 1.0 - jnp.power(BETA_ONE, step_float)
    fix_two = 1.0 - jnp.power(BETA_TWO, step_float)
    update = moment_new / fix_one / (jnp.sqrt(square_new / fix_two) + ADAM_EPS)
    master_new = master - rate_now * (update + DECAY * master)
    return (moment_new, square_new, master_new, master_new.astype(jnp.bfloat16))


def local(
    tables,
    lengths,
    cotangent,
    step_count,
    w_qkv,
    w_out,
    w_up,
    w_down,
    vectors,
    first_qkv,
    first_out,
    first_up,
    first_down,
    first_vec,
    second_qkv,
    second_out,
    second_up,
    second_down,
    second_vec,
):
    masters = (w_qkv, w_out, w_up, w_down, vectors)
    firsts = (first_qkv, first_out, first_up, first_down, first_vec)
    seconds = (second_qkv, second_out, second_up, second_down, second_vec)
    full_qkv, full_out, full_up, full_down, full_vec = (
        lax.all_gather(w_qkv.astype(jnp.bfloat16), "tab", axis=0, tiled=True),
        lax.all_gather(w_out.astype(jnp.bfloat16), "tab", axis=0, tiled=True),
        lax.all_gather(w_up.astype(jnp.bfloat16), "tab", axis=0, tiled=True),
        lax.all_gather(w_down.astype(jnp.bfloat16), "tab", axis=0, tiled=True),
        lax.all_gather(vectors.astype(jnp.bfloat16), "tab", axis=0, tiled=True),
    )
    vec_f = full_vec.astype(jnp.float32)
    bias_up = vec_f[:, 8:12].T.reshape(-1)
    table_count = tables.shape[0]
    local_len = tables.shape[1]
    scale_q = HD ** (-0.5)
    valid_keys = (
        lax.broadcasted_iota(jnp.int32, (table_count, 1, 1, LEN), 3) < lengths[:, None, None, None]
    )

    def score_block(query_h, key_h):
        raw_scores = (
            jnp.einsum("bqhd,bkhd->bhqk", query_h, key_h, preferred_element_type=jnp.float32)
            * scale_q
        )
        return jnp.where(valid_keys, raw_scores, NEGATIVE)

    tok_rows = tables.reshape(-1, D)
    proj_qkv = jnp.dot(tok_rows, full_qkv, preferred_element_type=jnp.float32)
    query_b = (proj_qkv[:, :D] + vec_f[:, 0]).astype(jnp.bfloat16)
    key_loc = proj_qkv[:, D : 2 * D].astype(jnp.bfloat16).reshape(table_count, local_len, D)
    value_loc = (
        (proj_qkv[:, 2 * D :] + vec_f[:, 1]).astype(jnp.bfloat16).reshape(table_count, local_len, D)
    )
    key_all, value_all = (
        lax.all_gather(key_loc, "blk", axis=1, tiled=True),
        lax.all_gather(value_loc, "blk", axis=1, tiled=True),
    )
    query_h = query_b.reshape(table_count, local_len, H, HD)
    key_h = key_all.reshape(table_count, LEN, H, HD)
    value_h = value_all.reshape(table_count, LEN, H, HD)
    scores = score_block(query_h, key_h)
    row_top = jnp.max(scores, axis=-1, keepdims=True)
    exp_scores = jnp.exp(scores - row_top)
    row_total = jnp.sum(exp_scores, axis=-1, keepdims=True)
    log_total = row_top + jnp.log(row_total)
    probs_b = (exp_scores / row_total).astype(jnp.bfloat16)
    mixed_heads = jnp.einsum(
        "bhqk,bkhd->bqhd", probs_b, value_h, preferred_element_type=jnp.float32
    )
    mixed_heads = mixed_heads.reshape(-1, D).astype(jnp.bfloat16)
    attn_out = jnp.dot(mixed_heads, full_out, preferred_element_type=jnp.float32) + vec_f[:, 2]
    normed_one, norm_one_back = jax.vjp(
        layer_norm, tok_rows.astype(jnp.float32) + attn_out, vec_f[:, 4], vec_f[:, 5]
    )
    normed_b = normed_one.astype(jnp.bfloat16)
    hidden = jnp.dot(normed_b, full_up, preferred_element_type=jnp.float32) + bias_up
    active, gelu_back = jax.vjp(partial(jax.nn.gelu, approximate=False), hidden)
    active_b = active.astype(jnp.bfloat16)
    branch = jnp.dot(active_b, full_down, preferred_element_type=jnp.float32) + vec_f[:, 3]
    result, norm_two_back = jax.vjp(layer_norm, normed_one + branch, vec_f[:, 6], vec_f[:, 7])
    output = result.astype(jnp.bfloat16).reshape(tables.shape)
    grad_out = cotangent.reshape(-1, D).astype(jnp.float32)
    grad_two, grad_g2, grad_c2 = norm_two_back(grad_out)
    grad_b2 = jnp.sum(grad_two, axis=0)
    branch_b = grad_two.astype(jnp.bfloat16)
    gw_down = inner(active_b, branch_b)
    grad_hidden = gelu_back(back_mul(branch_b, full_down))[0]
    grad_b1 = jnp.sum(grad_hidden, axis=0)
    hidden_b = grad_hidden.astype(jnp.bfloat16)
    gw_up = inner(normed_b, hidden_b)
    grad_one, grad_g1, grad_c1 = norm_one_back(grad_two + back_mul(hidden_b, full_up))
    grad_bo = jnp.sum(grad_one, axis=0)
    attn_b = grad_one.astype(jnp.bfloat16)
    gw_out = inner(mixed_heads, attn_b)
    grad_mixed = (
        back_mul(attn_b, full_out).astype(jnp.bfloat16).reshape(table_count, local_len, H, HD)
    )
    key_back, value_back = (
        lax.all_gather(key_loc, "blk", axis=1, tiled=True),
        lax.all_gather(value_loc, "blk", axis=1, tiled=True),
    )
    key_again = key_back.reshape(table_count, LEN, H, HD)
    value_again = value_back.reshape(table_count, LEN, H, HD)
    probs_again = jnp.exp(score_block(query_h, key_again) - log_total)
    grad_probs = jnp.einsum(
        "bqhd,bkhd->bhqk", grad_mixed, value_again, preferred_element_type=jnp.float32
    )
    row_dot = jnp.sum(grad_probs * probs_again, axis=-1, keepdims=True)
    grad_scores = (probs_again * (grad_probs - row_dot)).astype(jnp.bfloat16)
    grad_query = (
        jnp.einsum(
            "bhqk,bkhd->bqhd", grad_scores, key_again, preferred_element_type=jnp.float32
        ).reshape(-1, D)
        * scale_q
    )
    probs_again_b = probs_again.astype(jnp.bfloat16)
    part_key = (
        jnp.einsum(
            "bhqk,bqhd->bkhd", grad_scores, query_h, preferred_element_type=jnp.float32
        ).reshape(table_count, LEN, D)
        * scale_q
    )
    part_value = jnp.einsum(
        "bhqk,bqhd->bkhd", probs_again_b, grad_mixed, preferred_element_type=jnp.float32
    ).reshape(table_count, LEN, D)
    grad_key, grad_value = (
        lax.psum_scatter(
            part_key.astype(jnp.bfloat16), "blk", scatter_dimension=1, tiled=True
        ).astype(jnp.float32),
        lax.psum_scatter(
            part_value.astype(jnp.bfloat16), "blk", scatter_dimension=1, tiled=True
        ).astype(jnp.float32),
    )
    grad_key = grad_key.reshape(-1, D)
    grad_value = grad_value.reshape(-1, D)
    grad_bq = jnp.sum(grad_query, axis=0)
    grad_bv = jnp.sum(grad_value, axis=0)
    grad_qkv = jnp.concatenate([grad_query, grad_key, grad_value], axis=1).astype(jnp.bfloat16)
    gw_qkv = inner(tok_rows, grad_qkv)
    grad_input = grad_one + back_mul(grad_qkv, full_qkv)
    gw_vec = jnp.concatenate(
        [
            jnp.stack(
                [grad_bq, grad_bv, grad_bo, grad_b2, grad_g1, grad_c1, grad_g2, grad_c2], axis=1
            ),
            grad_b1.reshape(4, D).T,
        ],
        axis=1,
    )
    share_qkv, share_out, share_up, share_down, share_vec = (
        lax.psum_scatter(gw_qkv, "tab", scatter_dimension=0, tiled=True),
        lax.psum_scatter(gw_out, "tab", scatter_dimension=0, tiled=True),
        lax.psum_scatter(gw_up, "tab", scatter_dimension=0, tiled=True),
        lax.psum_scatter(gw_down, "tab", scatter_dimension=0, tiled=True),
        lax.psum_scatter(gw_vec, "tab", scatter_dimension=0, tiled=True),
    )
    shares = (
        lax.psum(share_qkv.astype(jnp.bfloat16), "blk").astype(jnp.float32),
        lax.psum(share_out.astype(jnp.bfloat16), "blk").astype(jnp.float32),
        lax.psum(share_up.astype(jnp.bfloat16), "blk").astype(jnp.float32),
        lax.psum(share_down.astype(jnp.bfloat16), "blk").astype(jnp.float32),
        lax.psum(share_vec.astype(jnp.bfloat16), "blk").astype(jnp.float32),
    )
    step_float = step_count[0].astype(jnp.float32)
    results = [output, grad_input.reshape(tables.shape)]
    for position in range(5):
        results.extend(
            adam(
                masters[position],
                shares[position],
                firsts[position],
                seconds[position],
                RATES[position],
                step_float,
            )
        )
    return tuple(results)


def solution(mesh):
    return jax.shard_map(
        local,
        mesh=mesh,
        in_specs=(
            P("tab", "blk", None),
            P("tab"),
            P("tab", "blk", None),
            P(),
            P("tab", None),
            P("tab", None),
            P("tab", None),
            P("tab", None),
            P("tab", None),
            P("tab", None),
            P("tab", None),
            P("tab", None),
            P("tab", None),
            P("tab", None),
            P("tab", None),
            P("tab", None),
            P("tab", None),
            P("tab", None),
            P("tab", None),
        ),
        out_specs=(
            P("tab", "blk", None),
            P("tab", "blk", None),
            P("tab", None),
            P("tab", None),
            P("tab", None),
            P("tab", None),
            P("tab", None),
            P("tab", None),
            P("tab", None),
            P("tab", None),
            P("tab", None),
            P("tab", None),
            P("tab", None),
            P("tab", None),
            P("tab", None),
            P("tab", None),
            P("tab", None),
            P("tab", None),
            P("tab", None),
            P("tab", None),
            P("tab", None),
            P("tab", None),
        ),
        check_vma=False,
    )
```

profile of v0, /device:TPU:0, one launch (start us, length us, event | category | flops | bytes accessed | tf_op | source)
XLA Modules:
  0.0 1251.9 jit_solution(16198308453331200462)
XLA Ops:
  9.3 68.8 %all-gather.8.cloned.1.call-done = bf16[768,2304]{1,0:T(8,128)(2,1)} async-done(((bf16[96,2304]{1,0:T(8,128)(2,1)}), bf16[768,2304]{1,0:T(8,128)(2,1)}) %all-gather.8.cloned.1.call-update) | async-done | bytes 3538960 | tf_op jit(solution)/shard_map/all_gather | solution.py:77
  89.4 30.6 %all-gather = bf16[8,96,12]{1,2,0:T(8,128)(2,1)S(1)} all-gather(bf16[1,96,12]{1,2,0:T(8,128)(2,1)S(1)} %convert_bitcast_fusion), channel_id=1, replica_groups=mesh['tab'=8,'blk'=4] {'tab'}, dimensions={0}, use_global_device_ids=true | all-gather | bytes 20736 | tf_op jit(solution)/shard_map/all_gather | solution.py:81
  134.6 8.6 copy.104
  143.3 12.9 %fusion.12 = (f32[8,12,128]{2,1,0:T(8,128)S(1)}, f32[8,12,128,512]{3,2,1,0:T(8,128)}) fusion(pred[8,512]{1,0:T(8,128)(4,1)S(1)} %iota_compare_fusion, bf16[8,512,12,64]{1,3,2,0:T(8,128)(2,1)} %bitcast.94, bf16[8,128,12,64]{1,0,3,2:T(8,128)(2,1)S(1)} %bitcast.99), kind=kOutput, calls=%fused_computation.29 | convolution fusion | flops 824168448 | bytes 33083392 | tf_op jit(solution)/shard_map/bqhd,bkhd->bhqk/dot_general | solution.py:94
  156.1 11.6 fusion
  168.4 14.7 %all-gather.10.cloned.1.call-done = bf16[8,512,768]{2,1,0:T(8,128)(2,1)} async-done(((bf16[8,128,768]{2,1,0:T(8,128)(2,1)}), bf16[8,512,768]{2,1,0:T(8,128)(2,1)}) %all-gather.10.cloned.1.call-update) | async-done | bytes 6291472 | tf_op jit(solution)/shard_map/all_gather | solution.py:108
  183.1 8.6 copy.102
  191.8 13.4 %fusion.35 = bf16[8,128,12,64]{1,3,2,0:T(8,128)(2,1)S(1)} fusion(bf16[8,512,12,64]{1,3,2,0:T(8,128)(2,1)} %bitcast.97, f32[8,12,128]{2,1,0:T(8,128)S(1)} %fusion, f32[8,12,128]{2,1,0:T(8,128)S(1)} %get-tuple-element.136, f32[8,12,128,512]{3,2,1,0:T(8,128)} %get-tuple-element.137, pred[8,512]{1,0:T(8,128)(4,1)S(1)} %iota_compare_fusion), kind=kOutput, calls=%fused_computation.79 | convolution fusion | flops 837550080 | bytes 33132544 | tf_op jit(solution)/shard_map/bhqk,bkhd->bqhd/dot_general | solution.py:119
  207.6 19.3 %all-gather.14.cloned.1.call-done = bf16[768,768]{1,0:T(8,128)(2,1)} async-done(((bf16[96,768]{1,0:T(8,128)(2,1)}), bf16[768,768]{1,0:T(8,128)(2,1)}) %all-gather.14.cloned.1.call-update) | async-done | bytes 1179664 | tf_op jit(solution)/shard_map/all_gather | solution.py:78
  231.3 76.3 %all-gather.16.cloned.1.call-done = bf16[768,3072]{1,0:T(8,128)(2,1)} async-done(((bf16[96,3072]{1,0:T(8,128)(2,1)}), bf16[768,3072]{1,0:T(8,128)(2,1)}) %all-gather.16.cloned.1.call-update) | async-done | bytes 4718608 | tf_op jit(solution)/shard_map/all_gather | solution.py:79
  307.6 36.0 %multiply_convert_fusion.2 = (bf16[1024,3072]{1,0:T(8,128)(2,1)}, f32[1024,3072]{1,0:T(8,128)}, f32[1024,3072]{1,0:T(8,128)}) fusion(f32[3072]{0:T(1024)S(1)} %add.223, bf16[768,3072]{1,0:T(8,128)(2,1)} %all-gather.16.cloned.1.call-done, f32[1024,768]{1,0:T(8,128)S(1)} %get-tuple-element.139, f32[768]{0:T(1024)S(1)} %get-tuple-element.96, ...), kind=kOutput, calls=%fused_computation.14 | convolution fusion | flops 5043388416 | bytes 39348224 | tf_op jit(solution)/shard_map/dot_general | solution.py:128
  343.6 44.3 %all-gather.18.cloned.1.call-done = bf16[3072,768]{1,0:T(8,128)(2,1)} async-done(((bf16[384,768]{1,0:T(8,128)(2,1)}), bf16[3072,768]{1,0:T(8,128)(2,1)}) %all-gather.18.cloned.1.call-update) | async-done | bytes 4718608 | tf_op jit(solution)/shard_map/all_gather | solution.py:80
  387.9 8.8 fusion.85
  403.0 19.2 %fusion.86 = (f32[3072]{0:T(1024)S(1)}, bf16[1024,3072]{1,0:T(8,128)(2,1)}) fusion(f32[1024,3072]{1,0:T(8,128)} %get-tuple-element.130, bf16[3072,768]{1,0:T(8,128)(2,1)} %all-gather.18.cloned.1.call-done, f32[1024,768]{1,0:T(8,128)} %get-tuple-element.128, f32[1024]{0:T(1024)S(1)} %negate_multiply_fusion.2, f32[1024,3072]{1,0:T(8,128)} %get-tuple-element.140, ...), kind=kOutput, calls=%fused_computation.151 | convolution fusion | flops 4883739648 | bytes 39350272 | tf_op jit(solution)/shard_map/dot_general | solution.py:37
  422.2 10.0 multiply_reduce_fusion.1
  442.5 13.1 %fusion.13 = bf16[8,12,64,512]{3,2,1,0:T(8,128)(2,1)} fusion(f32[8,12,128]{2,1,0:T(8,128)S(1)} %copy-done.24, f32[8,12,128,512]{3,2,1,0:T(8,128)} %get-tuple-element.137, pred[8,512]{1,0:T(8,128)(4,1)S(1)} %copy-done.26, bf16[8,128,12,64]{1,0,3,2:T(8,128)(2,1)S(1)} %bitcast.108), kind=kOutput, calls=%fused_computation.34 | convolution fusion | flops 833617920 | bytes 33083392 | tf_op jit(solution)/shard_map/bhqk,bqhd->bkhd/dot_general | solution.py:175
  455.6 8.7 copy.113
  464.3 24.1 %multiply_reduce_fusion = (f32[8,12,128]{2,1,0:T(8,128)S(1)}, f32[8,12,128,512]{3,2,1,0:T(8,128)}) fusion(f32[8,12,128]{2,1,0:T(8,128)S(1)} %copy-done.24, f32[8,12,128,512]{3,2,1,0:T(8,128)} %get-tuple-element.137, pred[8,512]{1,0:T(8,128)(4,1)S(1)} %copy-done.26, bf16[8,512,12,64]{1,3,2,0:T(8,128)(2,1)} %bitcast.98, bf16[8,128,12,64]{1,0,3,2:T(8,128)(2,1)} %bitcast.109), kind=kOutput, calls=%fused_computation.1 | convolution fusion | flops 836751360 | bytes 58298368 | tf_op jit(solution)/shard_map/bqhd,bkhd->bhqk/dot_general | solution.py:157
  488.5 17.0 %multiply_convert_fusion = bf16[8,12,128,512]{3,2,1,0:T(8,128)(2,1)S(1)} fusion(f32[8,12,128,512]{3,2,1,0:T(8,128)} %get-tuple-element.145, f32[8,12,128]{2,1,0:T(8,128)S(1)} %get-tuple-element.144, f32[8,12,128]{2,1,0:T(8,128)S(1)} %copy-done.24, f32[8,12,128,512]{3,2,1,0:T(8,128)} %get-tuple-element.137, pred[8,512]{1,0:T(8,128)(4,1)S(1)} %copy-done.26), kind=kLoop, calls=%fused_computation | loop fusion | flops 37748736 | bytes 63016960 | tf_op jit(solution)/shard_map/convert_element_type | solution.py:161
  511.9 8.7 copy.111
  526.2 10.8 fusion.22
  538.9 10.8 fusion.62
  550.0 10.8 multiply_reduce_fusion.5
  564.9 18.2 %reduce-scatter.12.cloned.1.call-done = bf16[8,128,768]{2,1,0:T(8,128)(2,1)} async-done(((bf16[8,512,768]{2,1,0:T(8,128)(2,1)}), bf16[8,128,768]{2,1,0:T(8,128)(2,1)}) %reduce-scatter.12.cloned.1.call-update) | async-done | bytes 1572880 | tf_op jit(solution)/shard_map/reduce_scatter | solution.py:179
  585.7 8.7 convolution_bitcast_fusion
  611.2 45.1 %reduce-scatter.16.cloned.1.call-done = f32[96,768]{1,0:T(8,128)} async-done(((f32[768,768]{1,0:T(8,128)}), f32[96,768]{1,0:T(8,128)}) %reduce-scatter.16.cloned.1.call-update) | async-done | bytes 294928 | tf_op jit(solution)/shard_map/reduce_scatter | solution.py:204
  657.9 163.1 %reduce-scatter.18.cloned.1.call-done = f32[96,3072]{1,0:T(8,128)} async-done(((f32[768,3072]{1,0:T(8,128)}), f32[96,3072]{1,0:T(8,128)}) %reduce-scatter.18.cloned.1.call-update) | async-done | bytes 1179664 | tf_op jit(solution)/shard_map/reduce_scatter | solution.py:205
  823.2 162.7 %reduce-scatter.20.cloned.1.call-done = f32[384,768]{1,0:T(8,128)} async-done(((f32[3072,768]{1,0:T(8,128)}), f32[384,768]{1,0:T(8,128)}) %reduce-scatter.20.cloned.1.call-update) | async-done | bytes 1179664 | tf_op jit(solution)/shard_map/reduce_scatter | solution.py:206
  988.0 130.0 %reduce-scatter.22.cloned.1.call-done = f32[96,2304]{1,0:T(8,128)} async-done(((f32[768,2304]{1,0:T(8,128)}), f32[96,2304]{1,0:T(8,128)}) %reduce-scatter.22.cloned.1.call-update) | async-done | bytes 884752 | tf_op jit(solution)/shard_map/reduce_scatter | solution.py:203
  1120.2 9.3 add_add_fusion.4
  1129.4 53.9 %reduce-scatter.24.cloned.1.call-done = f32[96,12]{1,0:T(8,128)} async-done(((f32[768,12]{1,0:T(8,128)}), f32[96,12]{1,0:T(8,128)}) %reduce-scatter.24.cloned.1.call-update) | async-done | bytes 4624
  1190.5 42.2 %all-reduce.3.cloned.1.call-done = (bf16[96,2304]{1,0:T(8,128)(2,1)}, bf16[96,768]{1,0:T(8,128)(2,1)}, bf16[96,3072]{1,0:T(8,128)(2,1)}, bf16[384,768]{1,0:T(8,128)(2,1)}) async-done(((bf16[96,2304]{1,0:T(8,128)(2,1)}, bf16[96,768]{1,0:T(8,128)(2,1)}, bf16[96,3072]{1,0:T(8,128)(2,1)}, bf16[384,768]{1,0:T(8,128)(2,1)}), (bf16[96,2304]{1,0:T(8,128)(2,1)}, bf16[96,768]{1,0:T(8,128)(2,1)}, ...) | async-done | bytes 1769488 | tf_op jit(solution)/shard_map/psum | solution.py:210
  (172 shorter events, 116.0 us)
Async XLA Ops:
  7.2 70.9 %all-gather.8.cloned.1.call-start = ((), (), s32[]{:S(2)}) async-start(), calls=%async_computation.7 | async-start | bytes 3981312 | tf_op jit(solution)/shard_map/all_gather | solution.py:77
  9.2 125.4 %all-gather.12.cloned.1.call-start = ((), (), s32[]{:S(2)}) async-start(), calls=%async_computation.9 | async-start | bytes 7864320 | tf_op jit(solution)/shard_map/all_gather | solution.py:107
  89.4 93.8 %all-gather.10.cloned.1.call-start = ((), (), s32[]{:S(2)}) async-start(), calls=%async_computation.8 | async-start | bytes 7864320 | tf_op jit(solution)/shard_map/all_gather | solution.py:108
  120.8 4.8 copy-start.20
  120.8 5.5 copy-start.11
  125.5 4.2 copy-start.35
  125.5 101.4 %all-gather.14.cloned.1.call-start = ((), (), s32[]{:S(2)}) async-start(), calls=%async_computation.10 | async-start | bytes 1327104 | tf_op jit(solution)/shard_map/all_gather | solution.py:78
  126.2 181.3 %all-gather.16.cloned.1.call-start = ((), (), s32[]{:S(2)}) async-start(), calls=%async_computation.11 | async-start | bytes 5308416 | tf_op jit(solution)/shard_map/all_gather | solution.py:79
  127.2 260.7 %all-gather.18.cloned.1.call-start = ((), (), s32[]{:S(2)}) async-start(), calls=%async_computation.12 | async-start | bytes 5308416 | tf_op jit(solution)/shard_map/all_gather | solution.py:80
  129.4 433.2 %reduce-scatter.14.cloned.1.call-start = ((), (), s32[]{:S(2)}) async-start(), calls=%async_computation.14 | async-start | bytes 7864320 | tf_op jit(solution)/shard_map/reduce_scatter | solution.py:182
  129.7 62.0 %copy-start.25 = (pred[8,512]{1,0:T(8,128)(4,1)}, pred[8,512]{1,0:T(8,128)(4,1)S(1)}, u32[]{:S(2)}) copy-start(pred[8,512]{1,0:T(8,128)(4,1)S(1)} %iota_compare_fusion) | copy-start | bytes 12292
  131.0 12.3 copy-start.1
  307.6 80.3 %copy-start.34 = (f32[768]{0:T(1024)S(1)}, f32[768]{0:T(1024)}, u32[]{:S(2)}) copy-start(f32[768]{0:T(1024)} %get-tuple-element.95) | copy-start | bytes 9220
  438.0 4.5 copy-start.24
  438.0 4.5 copy-start.26
  442.4 13.1 %copy-start.10 = (bf16[96,8,8,128]{3,2,1,0:T(8,128)(2,1)}, bf16[96,8,8,128]{3,2,1,0:T(8,128)(2,1)S(1)}, u32[]{:S(2)}) copy-start(bf16[96,8,8,128]{3,2,1,0:T(8,128)(2,1)S(1)} %copy.123) | copy-start | bytes 4718596
  464.3 118.8 %reduce-scatter.12.cloned.1.call-start = ((), (), s32[]{:S(2)}) async-start(), calls=%async_computation.13 | async-start | bytes 7864320 | tf_op jit(solution)/shard_map/reduce_scatter | solution.py:179
  488.5 17.1 %copy-start.2 = (bf16[96,8,8,128]{3,2,1,0:T(8,128)(2,1)S(1)}, bf16[96,8,8,128]{3,2,1,0:T(8,128)(2,1)}, u32[]{:S(2)}) copy-start(bf16[96,8,8,128]{3,2,1,0:T(8,128)(2,1)} %copy-done.1) | copy-start | bytes 4718596
  505.5 6.4 copy-start
  520.7 135.6 %reduce-scatter.16.cloned.1.call-start = ((), (), s32[]{:S(2)}) async-start(), calls=%async_computation.15 | async-start | bytes 2654208 | tf_op jit(solution)/shard_map/reduce_scatter | solution.py:204
  526.1 294.9 %reduce-scatter.18.cloned.1.call-start = ((), (), s32[]{:S(2)}) async-start(), calls=%async_computation.16 | async-start | bytes 10616832 | tf_op jit(solution)/shard_map/reduce_scatter | solution.py:205
  537.0 448.9 %reduce-scatter.20.cloned.1.call-start = ((), (), s32[]{:S(2)}) async-start(), calls=%async_computation.17 | async-start | bytes 10616832 | tf_op jit(solution)/shard_map/reduce_scatter | solution.py:206
  549.8 568.3 %reduce-scatter.22.cloned.1.call-start = ((), (), s32[]{:S(2)}) async-start(), calls=%async_computation.18 | async-start | bytes 7962624 | tf_op jit(solution)/shard_map/reduce_scatter | solution.py:203
  562.6 23.2 %copy-start.14 = (bf16[96,8,8,128]{3,1,2,0:T(8,128)(2,1)}, bf16[96,8,8,128]{3,1,2,0:T(8,128)(2,1)S(1)}, u32[]{:S(2)}) copy-start(bf16[96,8,8,128]{3,1,2,0:T(8,128)(2,1)S(1)} %copy.149) | copy-start | bytes 4718596
  564.9 29.5 %copy-start.15 = (bf16[1024,768]{0,1:T(8,128)(2,1)}, bf16[1024,768]{0,1:T(8,128)(2,1)S(1)}, u32[]{:S(2)}) copy-start(bf16[1024,768]{0,1:T(8,128)(2,1)S(1)} %copy.115) | copy-start | bytes 4718596
  602.5 580.8 %reduce-scatter.24.cloned.1.call-start = ((), (), s32[]{:S(2)}) async-start(), calls=%async_computation.19 | async-start | bytes 442368
  610.2 622.5 %all-reduce.3.cloned.1.call-start = ((), (), s32[]{:S(2)}) async-start(), calls=%async_computation.20 | async-start | bytes 3538944 | tf_op jit(solution)/shard_map/psum | solution.py:210
  657.9 462.2 %copy-start.6 = (f32[1024,768]{1,0:T(8,128)S(1)}, f32[1024,768]{1,0:T(8,128)}, u32[]{:S(2)}) copy-start(f32[1024,768]{1,0:T(8,128)} %copy-done.5) | copy-start | bytes 9437188
  1120.1 69.7 %copy-start.29 = (f32[96,12]{0,1:T(8,128)S(1)}, f32[96,12]{0,1:T(8,128)}, u32[]{:S(2)}) copy-start(f32[96,12]{0,1:T(8,128)} %param.27) | copy-start | bytes 13828
  1120.1 69.7 %copy-start.32 = (f32[96,12]{0,1:T(8,128)S(1)}, f32[96,12]{0,1:T(8,128)}, u32[]{:S(2)}) copy-start(f32[96,12]{0,1:T(8,128)} %param.37) | copy-start | bytes 13828
  1120.1 69.7 %copy-start.33 = (f32[96,12]{0,1:T(8,128)S(1)}, f32[96,12]{0,1:T(8,128)}, u32[]{:S(2)}) copy-start(f32[96,12]{0,1:T(8,128)} %param.32) | copy-start | bytes 13828
  1120.1 112.5 %copy-start.21 = (f32[96,768]{1,0:T(8,128)S(1)}, f32[96,768]{1,0:T(8,128)}, u32[]{:S(2)}) copy-start(f32[96,768]{1,0:T(8,128)} %param.24) | copy-start | bytes 884740
  (19 other events, 51.6 us)
Sparse Core Ops, SparseCore 0:
  10.8 67.3 all-gather.7
  89.5 45.0 all-gather.11
  136.8 46.3 all-gather.9
  185.8 41.1 all-gather.13
  229.5 77.9 all-gather.15
  310.2 77.6 all-gather.17
  464.4 57.2 reduce-scatter.13
  524.2 58.8 reduce-scatter.11
  586.6 69.6 reduce-scatter.15
  659.7 161.2 reduce-scatter.17
  824.7 161.2 reduce-scatter.19
  989.4 128.6 reduce-scatter.21
  1121.9 61.3 reduce-scatter.23
  1187.5 45.1 all-reduce.2
where the time goes:
time: 1260 us; the launch traced here: 1250 us
  waiting for transfers between devices  843 us (67%)
  matrix products  210 us (17%)
  local copies, waits for them, and re-layouts  74.5 us (6%)
  other arithmetic  71.6 us (6%)
  blocking collectives  36.3 us (3%)
  between operations  15.5 us (1%)
    reduce_scatter x1, waiting for transfers between devices, local(): lax.psum_scatter(gw_up, 'tab', scatter_dimension=0, tiled=True)  163 us
    reduce_scatter x1, waiting for transfers between devices, local(): lax.psum_scatter(gw_down, 'tab', scatter_dimension=0, tiled=True)  163 us
    reduce_scatter x1, waiting for transfers between devices, local(): lax.psum_scatter(gw_qkv, 'tab', scatter_dimension=0, tiled=True)  130 us
    all_gather x1, waiting for transfers between devices, local(): lax.all_gather(w_up.astype(jnp.bfloat16), 'tab', axis=0, tiled=True)  76.3 us
    all_gather x1, waiting for transfers between devices, local(): lax.all_gather(w_qkv.astype(jnp.bfloat16), 'tab', axis=0, tiled=True)  68.8 us
    unnamed x15, waiting for transfers between devices  54.1 us
    reduce_scatter x1, waiting for transfers between devices, local(): lax.psum_scatter(gw_out, 'tab', scatter_dimension=0, tiled=True)  45.1 us
    all_gather x1, waiting for transfers between devices, local(): lax.all_gather(w_down.astype(jnp.bfloat16), 'tab', axis=0, tiled=True)  44.3 us
  transfers between devices with their start and end apart: 14, of which 13 were waited for; matrix products, arithmetic and copies ran while one was open for 20% of the time, Pallas kernels for 0%

commit v1 on v0

v1 whole, which is shorter than its diff:
```python
from functools import partial

import jax
import jax.numpy as jnp
from jax import lax
from jax.experimental import pallas as pl
from jax.experimental.pallas import tpu as pltpu
from jax.sharding import PartitionSpec as P

D = 768
H = 12
HD = 64
LEN = 512
FF = 3072
PAIR = 2 * HD

EPS = 1e-06
NEGATIVE = -1e30
BETA_ONE = 0.9
BETA_TWO = 0.999
ADAM_EPS = 1e-08
DECAY = 0.01
RATES = (1.0, 15.0, 1.0, 0.5, 5.0)

F32 = jnp.float32
BF16 = jnp.bfloat16
MESH_ID = pl.DeviceIdType.MESH
VMEM_ALL = 64 * 1000 * 1024


def layer_norm(hidden, gain_vec, shift_vec):
    row_mean = jnp.mean(hidden, axis=-1, keepdims=True)
    centred = hidden - row_mean
    variance = jnp.mean(centred * centred, axis=-1, keepdims=True)
    return centred * lax.rsqrt(variance + EPS) * gain_vec + shift_vec


def inner(left, right):
    return lax.dot_general(left, right, (((0,), (0,)), ((), ())), preferred_element_type=F32)


def back_mul(left, right):
    return lax.dot_general(left, right, (((1,), (1,)), ((), ())), preferred_element_type=F32)


def adam(master, gradient, first_moment, second_moment, rate_now, step_float):
    moment_new = BETA_ONE * first_moment + (1.0 - BETA_ONE) * gradient
    square_new = BETA_TWO * second_moment + (1.0 - BETA_TWO) * gradient * gradient
    fix_one = 1.0 - jnp.power(BETA_ONE, step_float)
    fix_two = 1.0 - jnp.power(BETA_TWO, step_float)
    update = moment_new / fix_one / (jnp.sqrt(square_new / fix_two) + ADAM_EPS)
    master_new = master - rate_now * (update + DECAY * master)
    return (moment_new, square_new, master_new, master_new.astype(BF16))


def head_masks(dtype):
    lane = lax.broadcasted_iota(jnp.int32, (1, PAIR), 1)
    return [(lane < HD).astype(dtype), (lane >= HD).astype(dtype)]


def attn_fwd_kernel(len_ref, q_ref, k_ref, v_ref, o_ref, l_ref):
    live = len_ref[pl.program_id(0)]
    masks = head_masks(BF16)
    keys = k_ref[...]
    values = v_ref[...]
    rows = 256
    key_at = lax.broadcasted_iota(jnp.int32, (1, LEN), 1)
    bias = jnp.where(key_at < live, 0.0, NEGATIVE)
    lane = lax.broadcasted_iota(jnp.int32, (1, PAIR), 1)
    for start in range(0, LEN, rows):
        query = q_ref[pl.ds(start, rows), :] * jnp.asarray(HD ** (-0.5), BF16)
        mixed, logs = [], []
        for head in range(2):
            scores = back_mul(query * masks[head], keys) + bias
            top = jnp.max(scores, axis=-1, keepdims=True)
            raised = jnp.exp(scores - top)
            total = jnp.sum(raised, axis=-1, keepdims=True)
            probs = (raised * (1.0 / total)).astype(BF16)
            mixed.append(jnp.dot(probs, values, preferred_element_type=F32))
            logs.append(top + jnp.log(total))
        o_ref[pl.ds(start, rows), :] = jnp.where(lane < HD, mixed[0], mixed[1]).astype(BF16)
        both = jnp.where(lane < HD, logs[0], logs[1])
        flat = both.T
        l_ref[0, 0, 0:1, pl.ds(start, rows)] = flat[0:1, :]
        l_ref[0, 0, 1:2, pl.ds(start, rows)] = flat[HD : HD + 1, :]


def attention_forward(lengths, qkv, tables):
    pairs = H // 2
    spec = lambda part: pl.BlockSpec((LEN, PAIR), lambda t, h, n: (t, part * pairs + h))
    return pl.pallas_call(
        attn_fwd_kernel,
        grid_spec=pltpu.PrefetchScalarGridSpec(
            num_scalar_prefetch=1,
            grid=(tables, pairs),
            in_specs=[spec(0), spec(1), spec(2)],
            out_specs=[
                pl.BlockSpec((LEN, PAIR), lambda t, h, n: (t, h)),
                pl.BlockSpec((1, 1, 8, LEN), lambda t, h, n: (t, h, 0, 0)),
            ],
        ),
        out_shape=[
            jax.ShapeDtypeStruct((tables * LEN, D), BF16),
            jax.ShapeDtypeStruct((tables, pairs, 8, LEN), F32),
        ],
        name="attn_fwd",
    )(lengths, qkv, qkv, qkv)


def attn_bwd_kernel(len_ref, q_ref, k_ref, v_ref, o_ref, l_ref, do_ref, d_ref, sums_ref):
    live = len_ref[pl.program_id(0)]
    masks = head_masks(BF16)
    keys = k_ref[...]
    values = v_ref[...]
    query = q_ref[...] * jnp.asarray(HD ** (-0.5), BF16)
    grad_out = do_ref[...]
    dots = (grad_out.astype(F32) * o_ref[...].astype(F32)).T
    rows = 256
    q_masked = [query * m for m in masks]
    g_masked = [grad_out * m for m in masks]
    deltas = [jnp.sum(dots[h * HD : (h + 1) * HD, :], axis=0, keepdims=True) for h in range(2)]
    logs = [l_ref[0, 0, h : h + 1, :] for h in range(2)]
    grad_q = jnp.zeros((LEN, PAIR), F32)
    sum_v = jnp.zeros((1, PAIR), F32)
    for start in range(0, LEN, rows):
        part_k = keys[start : start + rows, :]
        part_v = values[start : start + rows, :]
        key_at = start + lax.broadcasted_iota(jnp.int32, (rows, 1), 0)
        bias = jnp.where(key_at < live, 0.0, NEGATIVE)
        grad_k = jnp.zeros((rows, PAIR), F32)
        grad_v = jnp.zeros((rows, PAIR), F32)
        for head in range(2):
            scores = back_mul(part_k, q_masked[head])
            probs = jnp.exp(scores + bias - logs[head])
            grad_probs = back_mul(part_v, g_masked[head])
            grad_s = (probs * (grad_probs - deltas[head])).astype(BF16)
            grad_v += jnp.dot(probs.astype(BF16), g_masked[head], preferred_element_type=F32)
            grad_k += jnp.dot(grad_s, q_masked[head], preferred_element_type=F32)
            grad_q += inner(grad_s, part_k * masks[head])
        d_ref[1, pl.ds(start, rows), :] = grad_k.astype(BF16)
        d_ref[2, pl.ds(start, rows), :] = grad_v.astype(BF16)
        sum_v += jnp.sum(grad_v, axis=0, keepdims=True)
    grad_q = grad_q * HD ** (-0.5)
    d_ref[0, :, :] = grad_q.astype(BF16)
    sums_ref[0, 0, 0:1, :] = jnp.sum(grad_q, axis=0, keepdims=True)
    sums_ref[0, 0, 1:2, :] = sum_v


def attention_backward(lengths, qkv, mixed, logs, grad_mixed, tables):
    pairs = H // 2
    spec = lambda part: pl.BlockSpec((LEN, PAIR), lambda t, h, n: (t, part * pairs + h))
    block = pl.BlockSpec((LEN, PAIR), lambda t, h, n: (t, h))
    return pl.pallas_call(
        attn_bwd_kernel,
        grid_spec=pltpu.PrefetchScalarGridSpec(
            num_scalar_prefetch=1,
            grid=(tables, pairs),
            in_specs=[
                spec(0),
                spec(1),
                spec(2),
                block,
                pl.BlockSpec((1, 1, 8, LEN), lambda t, h, n: (t, h, 0, 0)),
                block,
            ],
            out_specs=[
                pl.BlockSpec((3, LEN, PAIR), lambda t, h, n: (0, t, h)),
                pl.BlockSpec((1, 1, 8, PAIR), lambda t, h, n: (t, h, 0, 0)),
            ],
        ),
        out_shape=[
            jax.ShapeDtypeStruct((3, tables * LEN, D), BF16),
            jax.ShapeDtypeStruct((tables, pairs, 8, PAIR), F32),
        ],
        name="attn_bwd",
    )(lengths, qkv, qkv, qkv, mixed, logs, grad_mixed)


def place():
    tab, blk = lax.axis_index("tab"), lax.axis_index("blk")
    return tab // 2, tab % 2, blk // 2, blk % 2


class Wires:
    def __init__(self, send, recv):
        self.send, self.recv, self.count, self.sent = send, recv, 0, []

    def copy(self, src, dst, to):
        index, self.count = self.count, self.count + 1
        z, x, y, c = to
        made = pltpu.make_async_remote_copy(
            src_ref=src,
            dst_ref=dst,
            send_sem=self.send.at[index],
            recv_sem=self.recv.at[index],
            device_id=(z * 2 + x, y * 2 + c),
            device_id_type=MESH_ID,
        )
        made.start()
        self.sent.append(made)
        return made

    def finish(self):
        for made in self.sent:
            made.wait_send()


def greet(peers):
    barrier = pltpu.get_barrier_semaphore()
    for z, x, y, c in peers:
        pl.semaphore_signal(
            barrier, inc=1, device_id=(z * 2 + x, y * 2 + c), device_id_type=MESH_ID
        )
    pl.semaphore_wait(barrier, len(peers))


def all_peers():
    z, x, y, c = place()
    z_peers = [((z + j) % 4, x, y, c) for j in range(1, 4)]
    rest = [(z, 1 - x, y, c), (z, x, 1 - y, c), (z, x, y, 1 - c), (z, x, 1 - y, 1 - c)]
    return z_peers + rest


def by_columns(width):
    return lambda ref, t, part: ref.at[t, :, pl.ds(pl.multiple_of(part * width, 128), width)]


def by_rows(height):
    return lambda ref, t, part: ref.at[t, pl.ds(pl.multiple_of(part * height, 16), height), :]


PIECES = (
    (by_columns(FF // 4), True),
    (by_rows(FF // 32), True),
    (by_columns(3 * D // 2), False),
    (by_columns(D // 2), False),
)
N_WIRES = 160


def gather_kernel(
    x_in, cot_in, up_in, down_in, qkv_in, out_in, vec_in,
    x_out, cot_out, up_out, down_out, qkv_out, out_out, vec_out,
    send, recv, own,
):
    z, x, y, c = place()
    tab, blk = z * 2 + x, y * 2 + c
    greet(all_peers())
    wires = Wires(send, recv)
    shards = (up_in, down_in, qkv_in, out_in)
    wholes = (up_out, down_out, qkv_out, out_out)
    share, span = x_in.shape[0] // 4, x_in.shape[1]
    mine = pl.ds(blk * share, share)
    kept = [
        pltpu.make_async_copy(x_in.at[mine], x_out.at[:, pl.ds(blk * span, span), :], own.at[0]),
        pltpu.make_async_copy(cot_in.at[mine], cot_out.at[:, pl.ds(blk * span, span), :], own.at[1]),
        pltpu.make_async_copy(vec_in.at[0], vec_out.at[tab], own.at[2]),
    ]
    for at in range(4):
        kept.append(pltpu.make_async_copy(shards[at].at[0], wholes[at].at[tab], own.at[3 + at]))
    for made in kept:
        made.start()

    def trade(src, dst):
        made = []
        for other in ((z, x, 1 - y, c), (z, x, 1 - y, 1 - c), (z, x, y, 1 - c)):
            their = other[2] * 2 + other[3]
            made.append(
                wires.copy(
                    src.at[pl.ds(their * share, share)],
                    dst.at[:, pl.ds(blk * span, span), :],
                    other,
                )
            )
        return made

    waits = trade(x_in, x_out)
    along_z = []
    for at in range(4):
        piece, split = PIECES[at]
        part = blk if split else c
        along_z.append(
            [
                wires.copy(
                    piece(shards[at], 0, part),
                    piece(wholes[at], tab, part),
                    ((z + j) % 4, x, y, c),
                )
                for j in range(1, 4)
            ]
        )
    vec_z = [
        wires.copy(vec_in.at[0], vec_out.at[tab], ((z + j) % 4, x, y, c)) for j in range(1, 4)
    ]
    for at in range(4):
        piece, split = PIECES[at]
        whole = wholes[at]
        part = blk if split else c
        along_x, along_y = [], []

        def onward(t, local_part, kind):
            src = piece(whole, t, local_part)
            if kind == "y":
                along_y.append((t, wires.copy(src, src, (z, x, 1 - y, c))))
            else:
                waits.append(wires.copy(src, src, (z, x, y, 1 - c)))

        src = piece(shards[at], 0, part)
        along_x.append(wires.copy(src, piece(whole, tab, part), (z, 1 - x, y, c)))
        for j in range(1, 4):
            t = (z + 4 - j) % 4 * 2 + x
            along_z[at][j - 1].wait_recv()
            src = piece(whole, t, part)
            along_x.append(wires.copy(src, src, (z, 1 - x, y, c)))
            if split:
                onward(t, part, "y")
            onward(t, part, "c")
        for j in range(4):
            t = (z + 4 - j) % 4 * 2 + 1 - x
            along_x[j].wait_recv()
            if split:
                onward(t, part, "y")
            onward(t, part, "c")
        for t, made in along_y:
            made.wait_recv()
            onward(t, (1 - y) * 2 + c, "c")
    src = vec_in.at[0]
    vec_x = [wires.copy(src, vec_out.at[tab], (z, 1 - x, y, c))]
    for j in range(1, 4):
        t = (z + 4 - j) % 4 * 2 + x
        vec_z[j - 1].wait_recv()
        vec_x.append(wires.copy(vec_out.at[t], vec_out.at[t], (z, 1 - x, y, c)))
    waits += trade(cot_in, cot_out)
    for made in waits + vec_x:
        made.wait_recv()
    wires.finish()
    for made in kept:
        made.wait()


def gather_all(tables, cotangent, up, down, qkv, out, vec):
    share, span = tables.shape[0] // 4, tables.shape[1] * 4
    vmem = pl.BlockSpec(memory_space=pltpu.VMEM)
    hbm = pl.BlockSpec(memory_space=pl.ANY)
    shape = lambda a: jax.ShapeDtypeStruct((8,) + a.shape[1:], BF16)
    return pl.pallas_call(
        gather_kernel,
        in_specs=[vmem] * 7,
        out_specs=[hbm] * 7,
        out_shape=[
            jax.ShapeDtypeStruct((share, span, D), BF16),
            jax.ShapeDtypeStruct((share, span, D), BF16),
            shape(up), shape(down), shape(qkv), shape(out), shape(vec),
        ],
        scratch_shapes=[
            pltpu.SemaphoreType.DMA((N_WIRES,)),
            pltpu.SemaphoreType.DMA((N_WIRES,)),
            pltpu.SemaphoreType.DMA((7,)),
        ],
        compiler_params=pltpu.CompilerParams(
            collective_id=0, has_side_effects=True, vmem_limit_bytes=VMEM_ALL
        ),
        name="gather_all",
    )(tables, cotangent, up, down, qkv, out, vec)


class Plan:
    def __init__(self, send, recv):
        self.send, self.recv, self.makers = send, recv, []

    def add(self, maker):
        self.makers.append(maker)
        return len(self.makers) - 1

    def build(self, index):
        src, dst, (z, x, y, c) = self.makers[index]()
        return pltpu.make_async_remote_copy(
            src_ref=src,
            dst_ref=dst,
            send_sem=self.send.at[index],
            recv_sem=self.recv.at[index],
            device_id=(z * 2 + x, y * 2 + c),
            device_id_type=MESH_ID,
        )

    def start(self, index):
        self.build(index).start()

    def arrived(self, index):
        self.build(index).wait_recv()

    def finish(self):
        for index in range(len(self.makers)):
            self.build(index).wait_send()


class Slab:
    def __init__(self, rows, cols, split, axis, first=0, dtype=BF16):
        self.rows, self.cols, self.split, self.axis = rows, cols, split, axis
        self.first, self.dtype = first, dtype
        self.tile = 128 if axis == 1 else (16 if dtype == BF16 else 8)

    def cut(self, index):
        if self.axis == 1:
            return pl.ds(0, self.rows), pl.ds(
                pl.multiple_of(index * self.cols, self.tile), self.cols
            )
        start = pl.multiple_of(self.first + index * self.rows, self.tile)
        return pl.ds(start, self.rows), pl.ds(0, self.cols)

    def scratch(self):
        ways = 2 if self.split else 1
        vmem = lambda *lead: pltpu.VMEM(lead + (self.rows, self.cols), self.dtype)
        late = vmem(4, 2) if self.split else vmem(1, 1)
        return [vmem(ways, 4, 2), vmem(ways, 4, 2), late, vmem(4), vmem(3), vmem()]

    def copies(self):
        return (2 if self.split else 1) + 1 + 1 + 3 + 3


class Reduction:
    def __init__(self, slab, source, target, scratch, plan, own, own_at):
        self.slab, self.source, self.target, self.plan = slab, source, target, plan
        self.held, self.from_c, self.from_y, self.from_x, self.from_z, self.done = scratch
        self.own, self.own_at = own, own_at
        z, x, y, c = place()
        self.at = z, x, y, c
        self.slot = y if slab.split else 0
        side = (z, x, y, 1 - c)
        over = (z, x, 1 - y, c)

        def index_of(half, core):
            return half * 2 + core if slab.split else core

        def cut_all(ref, index):
            rows, cols = slab.cut(index)
            return ref.at[:, :, rows, cols]

        def cut_out(index):
            rows, cols = slab.cut(index)
            return target.at[rows, cols]

        ways = 2 if slab.split else 1
        self.loads = [
            lambda half=half: pltpu.make_async_copy(
                cut_all(source, index_of(half, c)), self.held.at[half], own.at[own_at + half]
            )
            for half in range(ways)
        ]
        self.to_core = [
            plan.add(
                lambda half=half: (
                    cut_all(source, index_of(half, 1 - c)), self.from_c.at[half], side,
                )
            )
            for half in range(ways)
        ]
        if slab.split:
            self.to_y = plan.add(lambda: (self.held.at[1 - y], self.from_y, over))
        else:
            self.to_y = plan.add(lambda: (self.done, self.from_y.at[0, 0], over))
        self.to_x = plan.add(
            lambda: (self.held.at[self.slot, :, 1 - x], self.from_x, (z, 1 - x, y, c))
        )
        self.to_z = [
            plan.add(
                lambda j=j: (
                    self.held.at[self.slot, (z + j) % 4, x],
                    self.from_z.at[j - 1],
                    ((z + j) % 4, x, y, c),
                )
            )
            for j in range(1, 4)
        ]
        mine = lambda: cut_out(index_of(y, c))
        self.store = lambda: pltpu.make_async_copy(self.done, mine(), own.at[own_at + 2])
        self.share_core = plan.add(lambda: (self.done, mine(), side))
        if slab.split:
            theirs = lambda: cut_out(index_of(1 - y, c))
            self.share_y = plan.add(lambda: (self.done, mine(), over))
            self.share_far = plan.add(lambda: (theirs(), theirs(), side))

    def begin(self):
        for load in self.loads:
            load().start()
        for index in self.to_core:
            self.plan.start(index)

    def summed(self, total, *others):
        value = total[...].astype(F32)
        for other in others:
            value = value + other[...].astype(F32)
        total[...] = value.astype(self.slab.dtype)

    def after_core(self):
        for half, load in enumerate(self.loads):
            load().wait()
            self.plan.arrived(self.to_core[half])

        def step(t, carry):
            for half in range(len(self.loads)):
                self.summed(self.held.at[half, t // 2, t % 2], self.from_c.at[half, t // 2, t % 2])
            return carry

        lax.fori_loop(0, 8, step, 0)
        self.plan.start(self.to_y if self.slab.split else self.to_x)

    def after_y(self):
        if not self.slab.split:
            return
        self.plan.arrived(self.to_y)

        def step(t, carry):
            self.summed(self.held.at[self.slot, t // 2, t % 2], self.from_y.at[t // 2, t % 2])
            return carry

        lax.fori_loop(0, 8, step, 0)
        self.plan.start(self.to_x)

    def after_x(self):
        z, x, y, c = self.at
        self.plan.arrived(self.to_x)

        def step(t, carry):
            self.summed(self.held.at[self.slot, t, x], self.from_x.at[t])
            return carry

        lax.fori_loop(0, 4, step, 0)
        for index in self.to_z:
            self.plan.start(index)

    def after_z(self):
        z, x, y, c = self.at
        for index in self.to_z:
            self.plan.arrived(index)
        value = self.held[self.slot, z, x].astype(F32)
        for j in range(3):
            value = value + self.from_z[j].astype(F32)
        self.done[...] = value.astype(self.slab.dtype)
        if self.slab.split:
            self.plan.start(self.share_y)
            self.plan.start(self.share_core)
            self.store().start()
        else:
            self.plan.start(self.to_y)

    def after_final(self):
        if self.slab.split:
            self.plan.arrived(self.share_y)
            self.plan.start(self.share_far)
        else:
            self.plan.arrived(self.to_y)
            self.plan.build(self.to_y).wait_send()
            self.summed(self.done, self.from_y.at[0, 0])
            self.plan.start(self.share_core)
            self.store().start()

    def end(self):
        self.plan.arrived(self.share_core)
        if self.slab.split:
            self.plan.arrived(self.share_far)
        self.store().wait()

    def finish_sends(self):
        done_early = () if self.slab.split else (self.to_y,)
        sends = self.to_core + [self.to_y, self.to_x] + self.to_z + [self.share_core]
        if self.slab.split:
            sends += [self.share_y, self.share_far]
        for index in sends:
            if index not in done_early:
                self.plan.build(index).wait_send()


STAGES = ("begin", "after_core", "after_y", "after_x", "after_z", "after_final", "end")

SLABS = (
    (0, Slab(96, FF // 4, True, 1)),
    (1, Slab(32, D, True, 0)),
    (1, Slab(128, D, False, 0, first=128)),
    (2, Slab(96, 3 * D // 2, False, 1)),
    (3, Slab(96, D // 2, False, 1)),
    (4, Slab(8, 128, False, 0, dtype=F32)),
)


def reduce_kernel(*refs):
    (gin_in, y_in), sources = refs[:2], refs[2:7]
    (gin_out, y_out), targets = refs[7:9], refs[9:14]
    scratch, (send, recv, own) = refs[14:-3], refs[-3:]
    z, x, y, c = place()
    blk = y * 2 + c
    greet(all_peers())
    plan = Plan(send, recv)
    share, span = gin_out.shape[0] // 4, gin_out.shape[1]
    kept, traded = [], []
    works = []
    for at, (number, slab) in enumerate(SLABS):
        part = scratch[6 * at : 6 * at + 6]
        works.append(
            Reduction(slab, sources[number], targets[number], part, plan, own, 2 + 3 * at)
        )
    for at, (src, dst) in enumerate(((gin_in, gin_out), (y_in, y_out))):
        mine = dst.at[pl.ds(blk * share, share)]
        kept.append(
            pltpu.make_async_copy(src.at[:, pl.ds(blk * span, span), :], mine, own.at[at])
        )
        kept[-1].start()
        for other in ((z, x, 1 - y, c), (z, x, 1 - y, 1 - c), (z, x, y, 1 - c)):
            their = other[2] * 2 + other[3]
            maker = lambda src=src, mine=mine, their=their, other=other: (
                src.at[:, pl.ds(their * span, span), :], mine, other,
            )
            traded.append(plan.add(maker))
    for stage in STAGES:
        for work in works:
            getattr(work, stage)()
        if stage == "after_y":
            for index in traded:
                plan.start(index)
    for index in traded:
        plan.arrived(index)
    for work in works:
        work.finish_sends()
    for index in traded:
        plan.build(index).wait_send()
    for made in kept:
        made.wait()


def reduce_all(grad_in, result, up, down, qkv, out, vec):
    share, length = grad_in.shape[:2]
    vmem = pl.BlockSpec(memory_space=pltpu.VMEM)
    hbm = pl.BlockSpec(memory_space=pl.ANY)
    shape = lambda a: jax.ShapeDtypeStruct(a.shape[2:], a.dtype)
    back = jax.ShapeDtypeStruct((share * 4, length // 4, D), BF16)
    grads = (up, down, qkv, out, vec)
    scratch = [s for _, slab in SLABS for s in slab.scratch()]
    wires = 6 + sum(slab.copies() for _, slab in SLABS)
    return pl.pallas_call(
        reduce_kernel,
        in_specs=[vmem] * 2 + [hbm] * 5,
        out_specs=[hbm] * 7,
        out_shape=[back, back] + [shape(a) for a in grads],
        scratch_shapes=scratch
        + [
            pltpu.SemaphoreType.DMA((wires,)),
            pltpu.SemaphoreType.DMA((wires,)),
            pltpu.SemaphoreType.DMA((2 + 3 * len(SLABS),)),
        ],
        compiler_params=pltpu.CompilerParams(
            collective_id=1, has_side_effects=True, vmem_limit_bytes=VMEM_ALL
        ),
        name="reduce_all",
    )(grad_in, result, *grads)


def local(*args):
    tables, lengths, cotangent, step_count = args[:4]
    masters, firsts, seconds = args[4:9], args[9:14], args[14:19]
    w_qkv, w_out, w_up, w_down, vectors = masters
    blocks = lax.axis_size("blk")
    shards = lax.axis_size("tab")
    table_count, local_len = tables.shape[:2]
    share = table_count // blocks
    tuned = shards == 8 and blocks == 4
    vec_pad = jnp.pad(vectors.astype(BF16).T, ((0, 4), (0, 128 - vectors.shape[0])))
    narrow = [w.astype(BF16) for w in (w_up, w_down, w_qkv, w_out)]
    if tuned:
        mine, cot, *wholes = gather_all(
            tables, cotangent, *[w[None] for w in narrow], vec_pad[None]
        )
    else:
        spread = partial(lax.all_to_all, axis_name="blk", split_axis=0, concat_axis=1, tiled=True)
        mine, cot = spread(tables), spread(cotangent)
        wholes = [lax.all_gather(w, "tab", axis=0) for w in narrow + [vec_pad]]
    full_up, full_down, full_qkv, full_out = [
        w.reshape(-1, w.shape[-1]) for w in wholes[:4]
    ]
    vec_f = wholes[4][:, :12, : vectors.shape[0]].transpose(1, 0, 2).reshape(12, D).astype(F32)
    my_lengths = lax.dynamic_slice(lengths, (lax.axis_index("blk") * share,), (share,))
    bias_up = vec_f[8:12].reshape(-1)
    bias_qkv = jnp.concatenate([vec_f[0], jnp.zeros((D,), F32), vec_f[1]])

    rows = mine.reshape(-1, D)
    qkv = (jnp.dot(rows, full_qkv, preferred_element_type=F32) + bias_qkv).astype(BF16)
    mixed, logs = attention_forward(my_lengths, qkv, share)
    attn_out = jnp.dot(mixed, full_out, preferred_element_type=F32) + vec_f[2]
    normed_one, norm_one_back = jax.vjp(
        layer_norm, rows.astype(F32) + attn_out, vec_f[4], vec_f[5]
    )
    normed_b = normed_one.astype(BF16)
    hidden = jnp.dot(normed_b, full_up, preferred_element_type=F32) + bias_up
    active, gelu_back = jax.vjp(partial(jax.nn.gelu, approximate=False), hidden)
    active_b = active.astype(BF16)
    branch = jnp.dot(active_b, full_down, preferred_element_type=F32) + vec_f[3]
    result, norm_two_back = jax.vjp(layer_norm, normed_one + branch, vec_f[6], vec_f[7])
    result = result.astype(BF16).reshape(mine.shape)
    grad_two, grad_g2, grad_c2 = norm_two_back(cot.reshape(-1, D).astype(F32))
    grad_b2 = jnp.sum(grad_two, axis=0)
    branch_b = grad_two.astype(BF16)
    gw_down = inner(active_b, branch_b).astype(BF16)
    grad_hidden = gelu_back(back_mul(branch_b, full_down))[0]
    grad_b1 = jnp.sum(grad_hidden, axis=0)
    hidden_b = grad_hidden.astype(BF16)
    gw_up = inner(normed_b, hidden_b).astype(BF16)
    grad_one, grad_g1, grad_c1 = norm_one_back(grad_two + back_mul(hidden_b, full_up))
    grad_bo = jnp.sum(grad_one, axis=0)
    attn_b = grad_one.astype(BF16)
    gw_out = inner(mixed, attn_b).astype(BF16)
    grad_mixed = back_mul(attn_b, full_out).astype(BF16)
    grad_three, sums = attention_backward(my_lengths, qkv, mixed, logs, grad_mixed, share)
    sums = jnp.sum(sums[:, :, :2], axis=0)
    grad_bq, grad_bv = sums[:, 0].reshape(-1), sums[:, 1].reshape(-1)
    grad_qkv = jnp.concatenate([grad_three[i] for i in range(3)], axis=1)
    gw_qkv = inner(rows, grad_qkv).astype(BF16)
    grad_in = grad_one + back_mul(grad_qkv, full_qkv)
    grad_in = grad_in.astype(BF16).reshape(mine.shape)
    gw_vec = jnp.concatenate(
        [
            jnp.stack([grad_bq, grad_bv, grad_bo, grad_b2, grad_g1, grad_c1, grad_g2, grad_c2]),
            grad_b1.reshape(4, D),
        ]
    )
    owned = vectors.shape[0]
    if tuned:
        pads = ((0, 0), (0, 0), (0, 2), (0, 128 - owned))
        wide_vec = jnp.pad(gw_vec.reshape(2, 6, shards, owned).transpose(2, 0, 1, 3), pads)
        by_owner = lambda g: g.reshape(4, 2, -1, g.shape[-1])
        grad_input, output, *sums = reduce_all(
            grad_in, result, by_owner(gw_up), by_owner(gw_down), by_owner(gw_qkv),
            by_owner(gw_out), wide_vec.reshape(4, 2, 16, 128),
        )
        sum_vec = sums[4].reshape(2, 8, 128)[:, :6, :owned].reshape(12, owned).T
        shares = [s.astype(F32) for s in (sums[2], sums[3], sums[0], sums[1], sum_vec)]
    else:
        back = partial(lax.all_to_all, axis_name="blk", split_axis=1, concat_axis=0, tiled=True)
        grad_input, output = back(grad_in), back(result)

        def collect(grad):
            part = lax.psum_scatter(
                grad.reshape(shards, -1, grad.shape[-1]), "tab", scatter_dimension=0
            )
            return lax.psum(part.astype(BF16), "blk").astype(F32)

        shares = [collect(g) for g in (gw_qkv, gw_out, gw_up, gw_down)]
        shares.append(collect(gw_vec.T.astype(BF16)))
    grad_input = grad_input.astype(F32)
    step_float = step_count[0].astype(F32)
    results = [output, grad_input]
    for at in range(5):
        results.extend(
            adam(masters[at], shares[at], firsts[at], seconds[at], RATES[at], step_float)
        )
    return tuple(results)


def solution(mesh):
    tokens, flat, rows = P("tab", "blk", None), P("tab"), P("tab", None)
    return jax.shard_map(
        local,
        mesh=mesh,
        in_specs=(tokens, flat, tokens, P()) + (rows,) * 15,
        out_specs=(tokens, tokens) + (rows,) * 20,
        check_vma=False,
    )
```

time: 1260 us -> 477 us (0.38)
  waiting for transfers between devices: 843 us -> 0 us
  Pallas kernels: 0 us -> 301 us
  matrix products: 210 us -> 122 us
  local copies, waits for them, and re-layouts: 74.5 us -> 12.5 us
  other arithmetic: 71.6 us -> 32.9 us
  blocking collectives: 36.3 us -> 0 us
  between operations: 15.5 us -> 2.14 us
    reduce_scatter x6 -> x0, waiting for transfers between devices: 519 us -> none  [the longest x1 163 us: local(): lax.psum_scatter(gw_up, 'tab', scatter_dimension=0, tiled=True)]
    pallas_call x0 -> x4, Pallas kernels: none -> 301 us  [the longest x1 134 us: reduce_all(): pl.pallas_call(reduce_kernel, in_specs=[vmem] * 2 + [hbm] * 5, out_specs=...]
    all_gather x6 -> x0, waiting for transfers between devices: 227 us -> none  [the longest x1 76.3 us: local(): lax.all_gather(w_up.astype(jnp.bfloat16), 'tab', axis=0, tiled=True)]
    dot_general x10 -> x4, matrix products: 133 us -> 53.1 us  [the longest x1 35.3 us: local(): hidden = jnp.dot(normed_b, full_up, preferred_element_type=F32) + bias_up]
    unnamed x15 -> x0, waiting for transfers between devices: 54.1 us -> none
    psum x1 -> x0, waiting for transfers between devices: 42.2 us -> none  [local(): lax.psum(share_qkv.astype(jnp.bfloat16), 'blk').astype(jnp.float32)]
    convert_element_type x16 -> x7, other arithmetic: 47.3 us -> 14.3 us  [the longest x5 11.6 us: adam(): return (moment_new, square_new, master_new, master_new.astype(BF16))]
    all_gather x1 -> x0, blocking collectives: 30.6 us -> none  [local(): lax.all_gather(vectors.astype(jnp.bfloat16), 'tab', axis=0, tiled=True)]
  transfers between devices with their start and end apart: 14 -> 0, of which waited for: 13 -> 0; matrix products, arithmetic and copies ran while one was open for 20% -> 0% of each run, Pallas kernels for 0% -> 0%
where the time goes in v1:
time: 477 us; the launch traced here: 470 us
  Pallas kernels  301 us (63%)
  matrix products  122 us (26%)
  other arithmetic  32.9 us (7%)
  local copies, waits for them, and re-layouts  12.5 us (3%)
    pallas_call x1, Pallas kernels, reduce_all(): pl.pallas_call(reduce_kernel, in_specs=[vmem] * 2 + [hbm] * 5, out_specs=...  134 us
    pallas_call x1, Pallas kernels, gather_all(): pl.pallas_call(gather_kernel, in_specs=[vmem] * 7, out_specs=[hbm] * 7, o...  116 us
    dot_general x4, matrix products, back_mul(): lax.dot_general(left, right, (((1,), (1,)), ((), ())), preferred_element_...  36.5 us
    dot_general x1, matrix products, local(): hidden = jnp.dot(normed_b, full_up, preferred_element_type=F32) + bias_up  35.3 us
    dot_general x4, matrix products, inner(): lax.dot_general(left, right, (((0,), (0,)), ((), ())), preferred_element_...  32.3 us
    pallas_call x1, Pallas kernels, attention_forward(): pl.pallas_call(attn_fwd_kernel, grid_spec=pltpu.PrefetchScalarGridSpec(nu...  25.8 us
    pallas_call x1, Pallas kernels, attention_backward(): pl.pallas_call(attn_bwd_kernel, grid_spec=pltpu.PrefetchScalarGridSpec(nu...  25.3 us
    convert_element_type x5, other arithmetic, adam(): return (moment_new, square_new, master_new, master_new.astype(BF16))  11.6 us

profile of v1, /device:TPU:0, one launch (start us, length us, event | category | flops | bytes accessed | tf_op | source)
XLA Modules:
  0.0 470.5 jit_solution(520489510381037946)
XLA Ops:
  1.5 1.2 dynamic_slice.3.len_ref
  4.0 1.6 convert_bitcast_fusion.3.out_in
  5.7 2.0 convert_bitcast_fusion.2.qkv_in
  7.7 2.2 convert_bitcast_fusion.1.up_in
  10.7 115.5 %gather_all.1 = (bf16[2,512,768]{2,1,0:T(8,128)(2,1)}, bf16[2,512,768]{2,1,0:T(8,128)(2,1)}, bf16[8,96,3072]{2,1,0:T(8,128)(2,1)}, bf16[8,384,768]{2,1,0:T(8,128...) custom-call(bf16[8,128,768]{2,1,0:T(8,128)(2,1)} %x_in.1, ...), custom_call_target="tpu_custom_call" | custom-call | tf_op jit(solution)/shard_map/gather_all/pallas_call | solution.py:346
  126.2 1.7 convert_reduce_fusion
  130.0 8.5 %add_convert_fusion.q_ref.k_ref.v_ref = bf16[1024,2304]{1,0:T(8,128)(2,1)} fusion(bf16[1024,768]{1,0:T(8,128)(2,1)} %bitcast.97, bf16[768,2304]{1,0:T(8,128)(2,1)} %bitcast.95, f32[2304]{0:T(1024)S(1)} %pad_maximum_fusion.5), kind=kOutput, calls=%fused_computation.17 | convolution fusion | flops 3628597248 | bytes 9839616 | tf_op jit(solution)/shard_map/dot_general | solution.py:685
  138.5 25.8 %attn_fwd.1 = (bf16[1024,768]{1,0:T(8,128)(2,1)}, f32[2,6,8,512]{3,2,1,0:T(8,128)}) custom-call(s32[2]{0:T(128)} %dynamic_slice.3.len_ref, bf16[1024,2304]{1,0:T(8,128)(2,1)} %add_convert_fusion.q_ref.k_ref.v_ref, bf16[1024,2304]{1,0:T(8,128)(2,1)} %add_convert_fusion.q_ref.k_ref.v_ref, bf16[1024,2304]{1,0:T(8,128)(2,1)} %add_convert_fusion.q_ref.k_ref.v_ref), custom_call_target="tpu_custom_call" | custom-call | tf_op jit(solution)/shard_map/attn_fwd/pallas_call | solution.py:91
  164.4 3.9 fusion.52
  168.8 35.3 %multiply_convert_fusion = (bf16[1024,3072]{1,0:T(8,128)(2,1)S(1)}, f32[1024,3072]{1,0:T(8,128)}, f32[1024,3072]{1,0:T(8,128)}) fusion(f32[3072]{0:T(1024)S(1)} %add.183, bf16[768,3072]{1,0:T(8,128)(2,1)S(1)} %bitcast.90, f32[1024,768]{1,0:T(8,128)S(1)} %get-tuple-element.104, f32[768]{0:T(1024)S(1)} %add.180, f32[768]{0:T(1024)S(1)} %mul.333, ...), kind=kOutput, calls=%fused_computation.3 | convolution fusion | flops 5043388416 | bytes 39348224 | tf_op jit(solution)/shard_map/dot_general | solution.py:692
  204.1 5.4 %fusion.53 = (f32[1024]{0:T(1024)S(1)}, f32[1024,768]{1,0:T(8,128)S(1)}) fusion(f32[768]{0:T(1024)S(1)} %add.186, bf16[1024,3072]{1,0:T(8,128)(2,1)S(1)} %get-tuple-element.95, bf16[3072,768]{1,0:T(8,128)(2,1)S(1)} %bitcast.94, f32[768]{0:T(1024)S(1)} %add.180, f32[768]{0:T(1024)S(1)} %mul.333, f32[1024]{0:T(1024)S(1)} %fusion.27, ...), kind=kOutput, calls=%fused_computation.120 | convolution fusion | flops 4837342208 | bytes 17323008 | tf_op jit(solution)/shard_map/dot_general | solution.py:695
  211.0 1.3 fusion.9
  212.3 3.1 fusion.50
  215.4 18.9 %fusion.54 = (f32[3072]{0:T(1024)S(1)}, bf16[1024,3072]{1,0:T(8,128)(2,1)}) fusion(f32[1024,3072]{1,0:T(8,128)} %get-tuple-element.96, bf16[3072,768]{1,0:T(8,128)(2,1)} %bitcast.91, f32[1024,768]{1,0:T(8,128)} %get-tuple-element.94, f32[1024]{0:T(1024)S(1)} %negate_multiply_fusion.2, f32[1024,3072]{1,0:T(8,128)} %get-tuple-element.105, f32[3072]{0:T(1024)S(1)} %add.183), kind=kOutput, calls=%fused_computation.121 | convolution fusion | flops 4883739648 | bytes 39350272 | tf_op jit(solution)/shard_map/dot_general | solution.py:43
  234.3 10.9 %convolution_convert_fusion = bf16[3072,768]{1,0:T(8,128)(2,1)} fusion(bf16[1024,3072]{1,0:T(8,128)(2,1)} %copy-done.29, f32[1024,768]{1,0:T(8,128)} %get-tuple-element.94, f32[1024]{0:T(1024)S(1)} %negate_multiply_fusion.2), kind=kOutput, calls=%fused_computation.18 | convolution fusion | flops 4835770368 | bytes 14159872 | tf_op jit(solution)/shard_map/dot_general | solution.py:39
  245.3 9.9 %multiply_reduce_fusion = (f32[768]{0:T(1024)S(1)}, f32[1024]{0:T(1024)S(1)}, f32[768]{0:T(1024)S(1)}, f32[1024,768]{1,0:T(8,128)}) fusion(f32[1024,768]{1,0:T(8,128)S(1)} %get-tuple-element.104, f32[1024]{0:T(1024)S(1)} %fusion.27, f32[1024]{0:T(1024)S(1)} %broadcast_multiply_fusion.1, f32[768]{0:T(1024)S(1)} %mul.333, bf16[768,3072]{1,0:T(8,128)(2,1)} %bitcast.87, ...), kind=kOutput, calls=%fused_computation.31 | convolution fusion | flops 4839699456 | bytes 20472832 | tf_op jit(solution)/shard_map/dot_general | solution.py:43
  255.9 2.8 fusion.49
  258.7 11.2 %convolution_convert_fusion.1 = bf16[768,3072]{1,0:T(8,128)(2,1)} fusion(bf16[1024,3072]{1,0:T(8,128)(2,1)} %get-tuple-element.110, f32[1024,768]{1,0:T(8,128)S(1)} %get-tuple-element.104, f32[768]{0:T(1024)S(1)} %add.180, f32[768]{0:T(1024)S(1)} %mul.333, f32[1024]{0:T(1024)S(1)} %fusion.27, f32[1024]{0:T(1024)S(1)} %broadcast_multiply_fusion.1), kind=kOutput, calls=%fused_computation.19 | convolution fusion | flops 4838129664 | bytes 14170112 | tf_op jit(solution)/shard_map/dot_general | solution.py:39
  270.3 0.9 copy-done.27
  271.2 2.7 convolution_convert_fusion.3.do_ref
  273.9 25.3 %attn_bwd.1 = (bf16[3,1024,768]{2,1,0:T(8,128)(2,1)}, f32[2,6,8,128]{3,2,1,0:T(8,128)}) custom-call(s32[2]{0:T(128)} %dynamic_slice.3.len_ref, bf16[1024,2304]{1,0:T(8,128)(2,1)} %add_convert_fusion.q_ref.k_ref.v_ref, bf16[1024,2304]{1,0:T(8,128)(2,1)} %add_convert_fusion.q_ref.k_ref.v_ref, bf16[1024,2304]{1,0:T(8,128)(2,1)} %add_convert_fusion.q_ref.k_ref.v_ref, ...), custom_call_target="tpu_custom_call" | custom-call | tf_op jit(solution)/shard_map/attn_bwd/pallas_call | solution.py:153
  299.2 4.1 convolution_convert_fusion.4
  303.6 1.7 copy-done.25
  305.3 5.0 %add_convert_fusion.2 = bf16[1024,768]{1,0:T(8,128)(2,1)} fusion(f32[1024,768]{1,0:T(8,128)S(1)} %copy-done.2, f32[1024]{0:T(1024)S(1)} %negate_multiply_fusion.1, bf16[768,2304]{1,0:T(8,128)(2,1)S(1)} %bitcast.96, bf16[1024,768]{1,0:T(8,128)(2,1)S(1)} %get-tuple-element.98, bf16[1024,768]{1,0:T(8,128)(2,1)S(1)} %get-tuple-element.99, ...), kind=kOutput, calls=%fused_computation.33 | convolution fusion | flops 3640393728 | bytes 12980224 | tf_op jit(solution)/shard_map/dot_general | solution.py:43
  310.3 6.0 %convolution_convert_fusion.2 = bf16[768,2304]{1,0:T(8,128)(2,1)} fusion(bf16[1024,768]{1,0:T(8,128)(2,1)S(1)} %bitcast.99, bf16[1024,768]{1,0:T(8,128)(2,1)S(1)} %get-tuple-element.98, bf16[1024,768]{1,0:T(8,128)(2,1)S(1)} %get-tuple-element.99, bf16[1024,768]{1,0:T(8,128)(2,1)S(1)} %get-tuple-element.97), kind=kOutput, calls=%fused_computation.20 | convolution fusion | flops 3639803904 | bytes 9830400 | tf_op jit(solution)/shard_map/dot_general | solution.py:39
  318.0 134.5 %reduce_all.1 = (bf16[8,128,768]{2,1,0:T(8,128)(2,1)}, bf16[8,128,768]{2,1,0:T(8,128)(2,1)}, bf16[96,3072]{1,0:T(8,128)(2,1)}, bf16[384,768]{1,0:T(8,128)(2,1)},...) custom-call(bf16[2,512,768]{2,1,0:T(8,128)(2,1)} %bitcast.82, ...), custom_call_target="tpu_custom_call" | custom-call | tf_op jit(solution)/shard_map/reduce_all/pallas_call | solution.py:639
  453.8 2.1 fusion.43
  455.9 3.7 fusion.46
  459.7 1.9 convert_element_type.135
  462.9 2.5 fusion.40
  466.5 2.6 fusion.37
  469.1 1.1 copy.50
  (114 shorter events, 12.9 us)
Async XLA Ops:
  0.7 9.2 %copy-start.5 = (f32[384,768]{1,0:T(8,128)S(1)}, f32[384,768]{1,0:T(8,128)}, u32[]{:S(2)}) copy-start(f32[384,768]{1,0:T(8,128)} %param.26) | copy-start | bytes 3538948
  164.3 4.5 slice-start
  164.3 4.5 slice-start.1
  164.3 39.8 %slice-start.2 = ((s8[4718592]{0:T(1024)(128)(4,1)}), s8[4194304]{0:T(1024)(128)(4,1)S(1)}, s32[]{:S(2)}) async-start(s8[4718592]{0:T(1024)(128)(4,1)} %bitcast.92), calls=%async_computation.2 | async-start | bytes 8388608
  168.8 35.3 %copy-start.19 = (f32[1024]{0:T(1024)}, f32[1024]{0:T(1024)S(1)}, u32[]{:S(2)}) copy-start(f32[1024]{0:T(1024)S(1)} %multiply_reduce_fusion.3) | copy-start | bytes 12292
  168.8 35.3 %slice-start.3 = ((s8[4718592]{0:T(1024)(128)(4,1)}), s8[524288]{0:T(1024)(128)(4,1)S(1)}, s32[]{:S(2)}) async-start(s8[4718592]{0:T(1024)(128)(4,1)} %bitcast.92), calls=%async_computation.3 | async-start | bytes 1048576
  204.1 5.5 %copy-start.29 = (bf16[1024,3072]{1,0:T(8,128)(2,1)}, bf16[1024,3072]{1,0:T(8,128)(2,1)S(1)}, u32[]{:S(2)}) copy-start(bf16[1024,3072]{1,0:T(8,128)(2,1)S(1)} %get-tuple-element.95) | copy-start | bytes 18874372
  209.6 1.4 copy-start
  234.3 11.0 %copy-start.3 = (f32[1024,768]{1,0:T(8,128)S(1)}, f32[1024,768]{1,0:T(8,128)}, u32[]{:S(2)}) copy-start(f32[1024,768]{1,0:T(8,128)} %get-tuple-element.94) | copy-start | bytes 9437188
  234.3 11.0 %copy-start.28 = (bf16[1024,3072]{1,0:T(8,128)(2,1)S(1)}, bf16[1024,3072]{1,0:T(8,128)(2,1)}, u32[]{:S(2)}) copy-start(bf16[1024,3072]{1,0:T(8,128)(2,1)} %get-tuple-element.110) | copy-start | bytes 18874372
  258.7 11.6 %copy-start.1 = (f32[1024,768]{1,0:T(8,128)}, f32[1024,768]{1,0:T(8,128)S(1)}, u32[]{:S(2)}) copy-start(f32[1024,768]{1,0:T(8,128)S(1)} %get-tuple-element.92) | copy-start | bytes 9437188
  273.9 25.3 %copy-start.2 = (f32[1024,768]{1,0:T(8,128)S(1)}, f32[1024,768]{1,0:T(8,128)}, u32[]{:S(2)}) copy-start(f32[1024,768]{1,0:T(8,128)} %copy-done.1) | copy-start | bytes 9437188
  299.2 4.1 copy-start.7
  303.3 2.0 copy-start.25
  305.3 5.0 %copy-start.26 = (bf16[2,512,768]{2,1,0:T(8,128)(2,1)S(1)}, bf16[2,512,768]{2,1,0:T(8,128)(2,1)}, u32[]{:S(2)}) copy-start(bf16[2,512,768]{2,1,0:T(8,128)(2,1)} %get-tuple-element.42) | copy-start | bytes 4718596
  310.3 6.8 %copy-start.22 = (f32[1,768]{1,0:T(1,128)S(1)}, f32[1,768]{1,0:T(1,128)}, u32[]{:S(2)}) copy-start(f32[1,768]{1,0:T(1,128)} %reshape.208) | copy-start | bytes 9220
  318.0 135.2 %copy-start.21 = (f32[96,12]{0,1:T(8,128)S(1)}, f32[96,12]{0,1:T(8,128)}, u32[]{:S(2)}) copy-start(f32[96,12]{0,1:T(8,128)} %param.27) | copy-start | bytes 13828
  318.0 135.2 %copy-start.23 = (f32[96,12]{0,1:T(8,128)S(1)}, f32[96,12]{0,1:T(8,128)}, u32[]{:S(2)}) copy-start(f32[96,12]{0,1:T(8,128)} %param.37) | copy-start | bytes 13828
  318.0 135.2 %copy-start.24 = (f32[96,12]{0,1:T(8,128)S(1)}, f32[96,12]{0,1:T(8,128)}, u32[]{:S(2)}) copy-start(f32[96,12]{0,1:T(8,128)} %param.32) | copy-start | bytes 13828
  318.0 135.8 %copy-start.15 = (f32[96,768]{1,0:T(8,128)S(1)}, f32[96,768]{1,0:T(8,128)}, u32[]{:S(2)}) copy-start(f32[96,768]{1,0:T(8,128)} %param.24) | copy-start | bytes 884740
  318.0 135.8 %copy-start.18 = (f32[96,768]{1,0:T(8,128)S(1)}, f32[96,768]{1,0:T(8,128)}, u32[]{:S(2)}) copy-start(f32[96,768]{1,0:T(8,128)} %param.34) | copy-start | bytes 884740
  318.0 138.0 %copy-start.8 = (f32[96,2304]{1,0:T(8,128)S(1)}, f32[96,2304]{1,0:T(8,128)}, u32[]{:S(2)}) copy-start(f32[96,2304]{1,0:T(8,128)} %param.23) | copy-start | bytes 2654212
  455.9 3.7 copy-start.10
  459.7 2.0 copy-start.4
  459.7 2.6 copy-start.11
  459.7 3.1 copy-start.12
  459.7 3.3 copy-start.17
  462.9 2.6 copy-start.6
  462.9 2.6 copy-start.13
  462.9 3.5 copy-start.14
  462.9 3.6 copy-start.16
  466.5 2.6 copy-start.9
  (2 other events, 2.0 us)

commit v2 on v1

--- a/solution.py
+++ b/solution.py
@@ -1,3 +1,4 @@
+import math
 from functools import partial
 
 import jax
@@ -690,8 +691,10 @@
     )
     normed_b = normed_one.astype(BF16)
     hidden = jnp.dot(normed_b, full_up, preferred_element_type=F32) + bias_up
-    active, gelu_back = jax.vjp(partial(jax.nn.gelu, approximate=False), hidden)
-    active_b = active.astype(BF16)
+    below = 0.5 * (1.0 + lax.erf(hidden * 0.5**0.5))
+    active_b = (hidden * below).astype(BF16)
+    slope = below + hidden * jnp.exp(-0.5 * hidden * hidden) * (2.0 * math.pi) ** -0.5
+    active_b, slope = lax.optimization_barrier((active_b, slope.astype(BF16)))
     branch = jnp.dot(active_b, full_down, preferred_element_type=F32) + vec_f[3]
     result, norm_two_back = jax.vjp(layer_norm, normed_one + branch, vec_f[6], vec_f[7])
     result = result.astype(BF16).reshape(mine.shape)
@@ -699,7 +702,7 @@
     grad_b2 = jnp.sum(grad_two, axis=0)
     branch_b = grad_two.astype(BF16)
     gw_down = inner(active_b, branch_b).astype(BF16)
-    grad_hidden = gelu_back(back_mul(branch_b, full_down))[0]
+    grad_hidden = back_mul(branch_b, full_down) * slope.astype(F32)
     grad_b1 = jnp.sum(grad_hidden, axis=0)
     hidden_b = grad_hidden.astype(BF16)
     gw_up = inner(normed_b, hidden_b).astype(BF16)

time: 477 us -> 448 us (0.939)
  matrix products: 122 us -> 92.8 us
    dot_general x1, matrix products: 35.3 us -> 13.3 us  [local(): hidden = jnp.dot(normed_b, full_up, preferred_element_type=F32) + bias_up]
    dot_general x4, matrix products: 36.5 us -> 30 us  [back_mul(): lax.dot_general(left, right, (((1,), (1,)), ((), ())), preferred_element_...]
where the time goes in v2:
time: 448 us; the launch traced here: 441 us
  Pallas kernels  301 us (67%)
  matrix products  92.8 us (21%)
  other arithmetic  32.8 us (7%)
  local copies, waits for them, and re-layouts  12.4 us (3%)
    pallas_call x1, Pallas kernels, reduce_all(): pl.pallas_call(reduce_kernel, in_specs=[vmem] * 2 + [hbm] * 5, out_specs=...  134 us
    pallas_call x1, Pallas kernels, gather_all(): pl.pallas_call(gather_kernel, in_specs=[vmem] * 7, out_specs=[hbm] * 7, o...  116 us
    dot_general x4, matrix products, inner(): lax.dot_general(left, right, (((0,), (0,)), ((), ())), preferred_element_...  31.6 us
    dot_general x4, matrix products, back_mul(): lax.dot_general(left, right, (((1,), (1,)), ((), ())), preferred_element_...  30 us
    pallas_call x1, Pallas kernels, attention_forward(): pl.pallas_call(attn_fwd_kernel, grid_spec=pltpu.PrefetchScalarGridSpec(nu...  25.8 us
    pallas_call x1, Pallas kernels, attention_backward(): pl.pallas_call(attn_bwd_kernel, grid_spec=pltpu.PrefetchScalarGridSpec(nu...  25.3 us
    dot_general x1, matrix products, local(): hidden = jnp.dot(normed_b, full_up, preferred_element_type=F32) + bias_up  13.3 us
    convert_element_type x5, other arithmetic, adam(): return (moment_new, square_new, master_new, master_new.astype(BF16))  11.6 us

profile of v2, /device:TPU:0, one launch (start us, length us, event | category | flops | bytes accessed | tf_op | source)
XLA Modules:
  0.0 441.0 jit_solution(13504174998781572395)
XLA Ops:
  1.5 1.2 dynamic_slice.3.len_ref
  4.0 1.6 convert_bitcast_fusion.3.out_in
  5.7 2.0 convert_bitcast_fusion.2.qkv_in
  7.7 2.2 convert_bitcast_fusion.1.up_in
  10.7 115.5 %gather_all.1 = (bf16[2,512,768]{2,1,0:T(8,128)(2,1)}, bf16[2,512,768]{2,1,0:T(8,128)(2,1)}, bf16[8,96,3072]{2,1,0:T(8,128)(2,1)}, bf16[8,384,768]{2,1,0:T(8,128...) custom-call(bf16[8,128,768]{2,1,0:T(8,128)(2,1)} %x_in.1, ...), custom_call_target="tpu_custom_call" | custom-call | tf_op jit(solution)/shard_map/gather_all/pallas_call | solution.py:347
  126.2 1.7 convert_reduce_fusion
  129.4 8.5 %add_convert_fusion.q_ref.k_ref.v_ref = bf16[1024,2304]{1,0:T(8,128)(2,1)} fusion(bf16[1024,768]{1,0:T(8,128)(2,1)} %bitcast.95, bf16[768,2304]{1,0:T(8,128)(2,1)} %bitcast.93, f32[2304]{0:T(1024)S(1)} %pad_maximum_fusion.5), kind=kOutput, calls=%fused_computation.9 | convolution fusion | flops 3628597248 | bytes 9839616 | tf_op jit(solution)/shard_map/dot_general | solution.py:686
  137.9 25.8 %attn_fwd.1 = (bf16[1024,768]{1,0:T(8,128)(2,1)}, f32[2,6,8,512]{3,2,1,0:T(8,128)}) custom-call(s32[2]{0:T(128)} %dynamic_slice.3.len_ref, bf16[1024,2304]{1,0:T(8,128)(2,1)} %add_convert_fusion.q_ref.k_ref.v_ref, bf16[1024,2304]{1,0:T(8,128)(2,1)} %add_convert_fusion.q_ref.k_ref.v_ref, bf16[1024,2304]{1,0:T(8,128)(2,1)} %add_convert_fusion.q_ref.k_ref.v_ref), custom_call_target="tpu_custom_call" | custom-call | tf_op jit(solution)/shard_map/attn_fwd/pallas_call | solution.py:92
  163.7 3.9 fusion.50
  168.2 13.3 %fusion.4 = (bf16[1024,3072]{1,0:T(8,128)(2,1)}, bf16[1024,3072]{1,0:T(8,128)(2,1)S(1)}) fusion(f32[3072]{0:T(1024)S(1)} %add.192, bf16[768,3072]{1,0:T(8,128)(2,1)S(1)} %bitcast.88, f32[1024,768]{1,0:T(8,128)S(1)} %get-tuple-element.108, f32[768]{0:T(1024)S(1)} %add.189, f32[768]{0:T(1024)S(1)} %mul.339, f32[1024]{0:T(1024)S(1)} %fusion.23, ...), kind=kOutput, calls=%fused_computation.5 | convolution fusion | flops 4873519104 | bytes 20473856 | tf_op jit(solution)/shard_map/dot_general | solution.py:693
  181.5 5.4 %fusion.51 = (f32[1024]{0:T(1024)S(1)}, f32[1024,768]{1,0:T(8,128)S(1)}) fusion(f32[768]{0:T(1024)S(1)} %add.198, bf16[1024,3072]{1,0:T(8,128)(2,1)S(1)} %get-tuple-element.49, bf16[3072,768]{1,0:T(8,128)(2,1)S(1)} %bitcast.91, f32[768]{0:T(1024)S(1)} %add.189, f32[768]{0:T(1024)S(1)} %mul.339, f32[1024]{0:T(1024)S(1)} %fusion.23, ...), kind=kOutput, calls=%fused_computation.112 | convolution fusion | flops 4837342208 | bytes 17323008 | tf_op jit(solution)/shard_map/dot_general | solution.py:698
  188.3 1.3 fusion.10
  189.6 2.6 fusion.49
  192.2 7.6 %convolution_convert_fusion = bf16[3072,768]{1,0:T(8,128)(2,1)} fusion(bf16[1024,3072]{1,0:T(8,128)(2,1)S(1)} %get-tuple-element.49, f32[1024,768]{1,0:T(8,128)S(1)} %get-tuple-element.98, f32[1024]{0:T(1024)S(1)} %negate_multiply_fusion.1), kind=kOutput, calls=%fused_computation.12 | convolution fusion | flops 4835770368 | bytes 14159872 | tf_op jit(solution)/shard_map/dot_general | solution.py:40
  200.1 10.0 %fusion.5 = (f32[3072]{0:T(1024)S(1)}, f32[1024,3072]{1,0:T(8,128)}) fusion(bf16[1024,3072]{1,0:T(8,128)(2,1)} %get-tuple-element.51, bf16[3072,768]{1,0:T(8,128)(2,1)S(1)} %bitcast.92, f32[1024,768]{1,0:T(8,128)S(1)} %get-tuple-element.98, f32[1024]{0:T(1024)S(1)} %negate_multiply_fusion.1), kind=kOutput, calls=%fused_computation.10 | convolution fusion | flops 4842845184 | bytes 26755072 | tf_op jit(solution)/shard_map/dot_general | solution.py:44
  210.1 12.4 %multiply_reduce_fusion = (f32[768]{0:T(1024)S(1)}, f32[1024]{0:T(1024)S(1)}, f32[768]{0:T(1024)S(1)}, f32[1024,768]{1,0:T(8,128)}) fusion(f32[1024,768]{1,0:T(8,128)S(1)} %get-tuple-element.108, f32[1024]{0:T(1024)S(1)} %fusion.23, f32[1024]{0:T(1024)S(1)} %broadcast_multiply_fusion.1, f32[768]{0:T(1024)S(1)} %mul.339, bf16[768,3072]{1,0:T(8,128)(2,1)} %bitcast.85, ...), kind=kOutput, calls=%fused_computation.25 | convolution fusion | flops 4849136640 | bytes 33055744 | tf_op jit(solution)/shard_map/dot_general | solution.py:44
  222.5 14.0 %convolution_convert_fusion.1 = bf16[768,3072]{1,0:T(8,128)(2,1)} fusion(f32[1024,3072]{1,0:T(8,128)} %get-tuple-element.113, bf16[1024,3072]{1,0:T(8,128)(2,1)} %get-tuple-element.51, f32[1024,768]{1,0:T(8,128)S(1)} %get-tuple-element.108, f32[768]{0:T(1024)S(1)} %add.189, f32[768]{0:T(1024)S(1)} %mul.339, f32[1024]{0:T(1024)S(1)} %fusion.23, ...), kind=kOutput, calls=%fused_computation.13 | convolution fusion | flops 4847566848 | bytes 26753024 | tf_op jit(solution)/shard_map/dot_general | solution.py:40
  236.5 3.2 fusion.48
  240.1 1.3 copy-done.1
  241.9 2.6 convolution_convert_fusion.3.do_ref
  244.5 25.3 %attn_bwd.1 = (bf16[3,1024,768]{2,1,0:T(8,128)(2,1)}, f32[2,6,8,128]{3,2,1,0:T(8,128)}) custom-call(s32[2]{0:T(128)} %dynamic_slice.3.len_ref, bf16[1024,2304]{1,0:T(8,128)(2,1)} %add_convert_fusion.q_ref.k_ref.v_ref, bf16[1024,2304]{1,0:T(8,128)(2,1)} %add_convert_fusion.q_ref.k_ref.v_ref, bf16[1024,2304]{1,0:T(8,128)(2,1)} %add_convert_fusion.q_ref.k_ref.v_ref, ...), custom_call_target="tpu_custom_call" | custom-call | tf_op jit(solution)/shard_map/attn_bwd/pallas_call | solution.py:154
  269.8 4.1 convolution_convert_fusion.4
  274.3 1.7 copy-done.21
  276.0 5.0 %add_convert_fusion.2 = bf16[1024,768]{1,0:T(8,128)(2,1)} fusion(f32[1024,768]{1,0:T(8,128)S(1)} %copy-done.2, f32[1024]{0:T(1024)S(1)} %negate_multiply_fusion, bf16[768,2304]{1,0:T(8,128)(2,1)S(1)} %bitcast.94, bf16[1024,768]{1,0:T(8,128)(2,1)S(1)} %get-tuple-element.102, bf16[1024,768]{1,0:T(8,128)(2,1)S(1)} %get-tuple-element.103, ...), kind=kOutput, calls=%fused_computation.27 | convolution fusion | flops 3640393728 | bytes 12980224 | tf_op jit(solution)/shard_map/dot_general | solution.py:44
  280.9 6.0 %convolution_convert_fusion.2 = bf16[768,2304]{1,0:T(8,128)(2,1)} fusion(bf16[1024,768]{1,0:T(8,128)(2,1)S(1)} %bitcast.97, bf16[1024,768]{1,0:T(8,128)(2,1)S(1)} %get-tuple-element.102, bf16[1024,768]{1,0:T(8,128)(2,1)S(1)} %get-tuple-element.103, bf16[1024,768]{1,0:T(8,128)(2,1)S(1)} %get-tuple-element.101), kind=kOutput, calls=%fused_computation.14 | convolution fusion | flops 3639803904 | bytes 9830400 | tf_op jit(solution)/shard_map/dot_general | solution.py:40
  288.6 134.4 %reduce_all.1 = (bf16[8,128,768]{2,1,0:T(8,128)(2,1)}, bf16[8,128,768]{2,1,0:T(8,128)(2,1)}, bf16[96,3072]{1,0:T(8,128)(2,1)}, bf16[384,768]{1,0:T(8,128)(2,1)},...) custom-call(bf16[2,512,768]{2,1,0:T(8,128)(2,1)} %bitcast.80, ...), custom_call_target="tpu_custom_call" | custom-call | tf_op jit(solution)/shard_map/reduce_all/pallas_call | solution.py:640
  424.4 2.1 fusion.42
  426.5 3.7 fusion.45
  430.3 1.9 convert_element_type.143
  433.5 2.5 fusion.39
  437.1 2.6 fusion.36
  439.7 1.1 copy.50
  (102 shorter events, 12.4 us)
Async XLA Ops:
  0.7 9.2 %copy-start.4 = (f32[384,768]{1,0:T(8,128)S(1)}, f32[384,768]{1,0:T(8,128)}, u32[]{:S(2)}) copy-start(f32[384,768]{1,0:T(8,128)} %param.26) | copy-start | bytes 3538948
  163.7 4.4 %slice-start = ((s8[4718592]{0:T(1024)(128)(4,1)}), s8[4194304]{0:T(1024)(128)(4,1)S(1)}, s32[]{:S(2)}) async-start(s8[4718592]{0:T(1024)(128)(4,1)} %bitcast.86), calls=%async_computation | async-start | bytes 8388608
  163.7 4.4 %slice-start.1 = ((s8[4718592]{0:T(1024)(128)(4,1)}), s8[524288]{0:T(1024)(128)(4,1)S(1)}, s32[]{:S(2)}) async-start(s8[4718592]{0:T(1024)(128)(4,1)} %bitcast.86), calls=%async_computation.1 | async-start | bytes 1048576
  167.6 13.8 %slice-start.2 = ((s8[4718592]{0:T(1024)(128)(4,1)}), s8[4194304]{0:T(1024)(128)(4,1)S(1)}, s32[]{:S(2)}) async-start(s8[4718592]{0:T(1024)(128)(4,1)} %bitcast.89), calls=%async_computation.2 | async-start | bytes 8388608
  168.2 13.3 %slice-start.3 = ((s8[4718592]{0:T(1024)(128)(4,1)}), s8[524288]{0:T(1024)(128)(4,1)S(1)}, s32[]{:S(2)}) async-start(s8[4718592]{0:T(1024)(128)(4,1)} %bitcast.89), calls=%async_computation.3 | async-start | bytes 1048576
  186.9 1.4 copy-start
  239.7 1.7 copy-start.1
  239.7 2.1 copy-start.23
  244.5 25.3 %copy-start.2 = (f32[1024,768]{1,0:T(8,128)S(1)}, f32[1024,768]{1,0:T(8,128)}, u32[]{:S(2)}) copy-start(f32[1024,768]{1,0:T(8,128)} %copy-done.1) | copy-start | bytes 9437188
  269.8 4.1 copy-start.6
  274.0 2.0 copy-start.21
  276.0 5.0 %copy-start.22 = (bf16[2,512,768]{2,1,0:T(8,128)(2,1)S(1)}, bf16[2,512,768]{2,1,0:T(8,128)(2,1)}, u32[]{:S(2)}) copy-start(bf16[2,512,768]{2,1,0:T(8,128)(2,1)} %get-tuple-element.44) | copy-start | bytes 4718596
  288.6 135.2 %copy-start.18 = (f32[96,12]{0,1:T(8,128)S(1)}, f32[96,12]{0,1:T(8,128)}, u32[]{:S(2)}) copy-start(f32[96,12]{0,1:T(8,128)} %param.27) | copy-start | bytes 13828
  288.6 135.2 %copy-start.19 = (f32[96,12]{0,1:T(8,128)S(1)}, f32[96,12]{0,1:T(8,128)}, u32[]{:S(2)}) copy-start(f32[96,12]{0,1:T(8,128)} %param.37) | copy-start | bytes 13828
  288.6 135.2 %copy-start.20 = (f32[96,12]{0,1:T(8,128)S(1)}, f32[96,12]{0,1:T(8,128)}, u32[]{:S(2)}) copy-start(f32[96,12]{0,1:T(8,128)} %param.32) | copy-start | bytes 13828
  288.6 135.8 %copy-start.14 = (f32[96,768]{1,0:T(8,128)S(1)}, f32[96,768]{1,0:T(8,128)}, u32[]{:S(2)}) copy-start(f32[96,768]{1,0:T(8,128)} %param.24) | copy-start | bytes 884740
  288.6 135.8 %copy-start.17 = (f32[96,768]{1,0:T(8,128)S(1)}, f32[96,768]{1,0:T(8,128)}, u32[]{:S(2)}) copy-start(f32[96,768]{1,0:T(8,128)} %param.34) | copy-start | bytes 884740
  288.6 137.9 %copy-start.7 = (f32[96,2304]{1,0:T(8,128)S(1)}, f32[96,2304]{1,0:T(8,128)}, u32[]{:S(2)}) copy-start(f32[96,2304]{1,0:T(8,128)} %param.23) | copy-start | bytes 2654212
  426.5 3.7 copy-start.9
  430.2 2.0 copy-start.3
  430.2 2.6 copy-start.10
  430.2 3.1 copy-start.11
  430.3 3.3 copy-start.16
  433.5 2.6 copy-start.5
  433.5 2.6 copy-start.12
  433.5 3.5 copy-start.13
  433.5 3.6 copy-start.15
  437.1 2.6 copy-start.8

commit v3 on v2

--- a/solution.py
+++ b/solution.py
@@ -182,30 +182,6 @@
     return tab // 2, tab % 2, blk // 2, blk % 2
 
 
-class Wires:
-    def __init__(self, send, recv):
-        self.send, self.recv, self.count, self.sent = send, recv, 0, []
-
-    def copy(self, src, dst, to):
-        index, self.count = self.count, self.count + 1
-        z, x, y, c = to
-        made = pltpu.make_async_remote_copy(
-            src_ref=src,
-            dst_ref=dst,
-            send_sem=self.send.at[index],
-            recv_sem=self.recv.at[index],
-            device_id=(z * 2 + x, y * 2 + c),
-            device_id_type=MESH_ID,
-        )
-        made.start()
-        self.sent.append(made)
-        return made
-
-    def finish(self):
-        for made in self.sent:
-            made.wait_send()
-
-
 def greet(peers):
     barrier = pltpu.get_barrier_semaphore()
     for z, x, y, c in peers:
@@ -231,138 +207,288 @@
 
 
 PIECES = (
-    (by_columns(FF // 4), True),
-    (by_rows(FF // 32), True),
     (by_columns(3 * D // 2), False),
     (by_columns(D // 2), False),
+    (by_columns(FF // 4), True),
+    (by_rows(FF // 16), False),
 )
-N_WIRES = 160
+G_WIRES = 96
+STEPS = 12
+
+
+class Gather:
+    def __init__(self, at, shard, whole, plan):
+        piece, self.split = PIECES[at]
+        z, x, y, c = place()
+        tab = z * 2 + x
+        part = y * 2 + c if self.split else c
+        other = (1 - y) * 2 + c
+        own = lambda: piece(shard, 0, part)
+        self.plan = plan
+        near = lambda j: (z + 4 - j) % 4 * 2 + x
+        far = lambda j: (z + 4 - j) % 4 * 2 + 1 - x
+
+        def send(at_tab, which, to, first=False):
+            return plan.add(
+                lambda: (
+                    own() if first else piece(whole, at_tab, which),
+                    piece(whole, at_tab, which),
+                    to,
+                )
+            )
+
+        side, over, across = (z, x, y, 1 - c), (z, x, 1 - y, c), (z, 1 - x, y, c)
+        self.z = [send(tab, part, ((z + j) % 4, x, y, c), True) for j in range(1, 4)]
+        self.x = [send(tab, part, across, True)]
+        self.x += [send(near(j), part, across) for j in range(1, 4)]
+        tabs = [near(j) for j in range(1, 4)] + [far(j) for j in range(4)]
+        self.c = [send(t, part, side) for t in tabs]
+        self.y = [send(t, part, over) for t in tabs] if self.split else []
+        self.late = [send(t, other, side) for t in tabs] if self.split else []
+
+    def send_z(self):
+        for index in self.z:
+            self.plan.start(index)
+
+    def send_x(self):
+        self.plan.start(self.x[0])
+
+    def onward(self, at):
+        if self.split:
+            self.plan.start(self.y[at])
+        self.plan.start(self.c[at])
+
+    def task_z(self, j):
+        self.plan.arrived(self.z[j - 1])
+        self.plan.start(self.x[j])
+        self.onward(j - 1)
+
+    def task_x(self, j):
+        self.plan.arrived(self.x[j])
+        self.onward(3 + j)
+
+    def task_y(self, at):
+        self.plan.arrived(self.y[at])
+        self.plan.start(self.late[at])
+
+    def end(self):
+        for index in self.c + self.late:
+            self.plan.arrived(index)
 
 
 def gather_kernel(
-    x_in, cot_in, up_in, down_in, qkv_in, out_in, vec_in,
-    x_out, cot_out, up_out, down_out, qkv_out, out_out, vec_out,
-    send, recv, own,
+    len_ref, x_in, cot_in, qkv_in, out_in, up_in, down_in, vec_in,
+    x_out, cot_out, qkv_out, out_out, up_out, down_out, vec_out, acts_out, mixed_out, logs_out,
+    x_all, w_all, vec_all, acts, mixed, logs, send, recv, own,
 ):
     z, x, y, c = place()
     tab, blk = z * 2 + x, y * 2 + c
-    greet(all_peers())
-    wires = Wires(send, recv)
-    shards = (up_in, down_in, qkv_in, out_in)
-    wholes = (up_out, down_out, qkv_out, out_out)
     share, span = x_in.shape[0] // 4, x_in.shape[1]
     mine = pl.ds(blk * share, share)
-    kept = [
-        pltpu.make_async_copy(x_in.at[mine], x_out.at[:, pl.ds(blk * span, span), :], own.at[0]),
-        pltpu.make_async_copy(cot_in.at[mine], cot_out.at[:, pl.ds(blk * span, span), :], own.at[1]),
-        pltpu.make_async_copy(vec_in.at[0], vec_out.at[tab], own.at[2]),
-    ]
-    for at in range(4):
-        kept.append(pltpu.make_async_copy(shards[at].at[0], wholes[at].at[tab], own.at[3 + at]))
-    for made in kept:
-        made.start()
+    slot = pl.ds(pl.multiple_of(blk * span, span), span)
+    plan = Plan(send, recv)
+    shards = (qkv_in, out_in, up_in, down_in)
+    wholes = (w_all, out_out, up_out, down_out)
+    works = [Gather(at, shards[at], wholes[at], plan) for at in range(4)]
+    qkv, out, up, down = works
 
     def trade(src, dst):
         made = []
         for other in ((z, x, 1 - y, c), (z, x, 1 - y, 1 - c), (z, x, y, 1 - c)):
             their = other[2] * 2 + other[3]
             made.append(
-                wires.copy(
-                    src.at[pl.ds(their * share, share)],
-                    dst.at[:, pl.ds(blk * span, span), :],
-                    other,
+                plan.add(
+                    lambda their=their, other=other: (
+                        src.at[pl.ds(their * share, share)], dst.at[:, slot, :], other,
+                    )
                 )
             )
         return made
 
-    waits = trade(x_in, x_out)
-    along_z = []
-    for at in range(4):
-        piece, split = PIECES[at]
-        part = blk if split else c
-        along_z.append(
-            [
-                wires.copy(
-                    piece(shards[at], 0, part),
-                    piece(wholes[at], tab, part),
-                    ((z + j) % 4, x, y, c),
-                )
-                for j in range(1, 4)
-            ]
-        )
+    trade_x, trade_cot = trade(x_in, x_all), trade(cot_in, cot_out)
     vec_z = [
-        wires.copy(vec_in.at[0], vec_out.at[tab], ((z + j) % 4, x, y, c)) for j in range(1, 4)
+        plan.add(lambda j=j: (vec_in.at[0], vec_all.at[tab], ((z + j) % 4, x, y, c)))
+        for j in range(1, 4)
     ]
-    for at in range(4):
-        piece, split = PIECES[at]
-        whole = wholes[at]
-        part = blk if split else c
-        along_x, along_y = [], []
-
-        def onward(t, local_part, kind):
-            src = piece(whole, t, local_part)
-            if kind == "y":
-                along_y.append((t, wires.copy(src, src, (z, x, 1 - y, c))))
-            else:
-                waits.append(wires.copy(src, src, (z, x, y, 1 - c)))
-
-        src = piece(shards[at], 0, part)
-        along_x.append(wires.copy(src, piece(whole, tab, part), (z, 1 - x, y, c)))
-        for j in range(1, 4):
-            t = (z + 4 - j) % 4 * 2 + x
-            along_z[at][j - 1].wait_recv()
-            src = piece(whole, t, part)
-            along_x.append(wires.copy(src, src, (z, 1 - x, y, c)))
-            if split:
-                onward(t, part, "y")
-            onward(t, part, "c")
-        for j in range(4):
-            t = (z + 4 - j) % 4 * 2 + 1 - x
-            along_x[j].wait_recv()
-            if split:
-                onward(t, part, "y")
-            onward(t, part, "c")
-        for t, made in along_y:
-            made.wait_recv()
-            onward(t, (1 - y) * 2 + c, "c")
-    src = vec_in.at[0]
-    vec_x = [wires.copy(src, vec_out.at[tab], (z, 1 - x, y, c))]
+    vec_x = [plan.add(lambda: (vec_in.at[0], vec_all.at[tab], (z, 1 - x, y, c)))]
     for j in range(1, 4):
         t = (z + 4 - j) % 4 * 2 + x
-        vec_z[j - 1].wait_recv()
-        vec_x.append(wires.copy(vec_out.at[t], vec_out.at[t], (z, 1 - x, y, c)))
-    waits += trade(cot_in, cot_out)
-    for made in waits + vec_x:
-        made.wait_recv()
-    wires.finish()
-    for made in kept:
-        made.wait()
-
-
-def gather_all(tables, cotangent, up, down, qkv, out, vec):
+        vec_x.append(plan.add(lambda t=t: (vec_all.at[t], vec_all.at[t], (z, 1 - x, y, c))))
+    keeps = [
+        lambda: pltpu.make_async_copy(x_in.at[mine], x_all.at[:, slot, :], own.at[0]),
+        lambda: pltpu.make_async_copy(qkv_in.at[0], w_all.at[tab], own.at[1]),
+        lambda: pltpu.make_async_copy(vec_in.at[0], vec_all.at[tab], own.at[2]),
+        lambda: pltpu.make_async_copy(cot_in.at[mine], cot_out.at[:, slot, :], own.at[3]),
+        lambda: pltpu.make_async_copy(out_in.at[0], out_out.at[tab], own.at[4]),
+        lambda: pltpu.make_async_copy(up_in.at[0], up_out.at[tab], own.at[5]),
+        lambda: pltpu.make_async_copy(down_in.at[0], down_out.at[tab], own.at[6]),
+    ]
+    puts = [
+        lambda: pltpu.make_async_copy(x_all, x_out, own.at[7]),
+        lambda: pltpu.make_async_copy(w_all, qkv_out, own.at[8]),
+        lambda: pltpu.make_async_copy(vec_all, vec_out, own.at[9]),
+        lambda: pltpu.make_async_copy(acts, acts_out, own.at[10]),
+        lambda: pltpu.make_async_copy(mixed, mixed_out, own.at[11]),
+        lambda: pltpu.make_async_copy(logs, logs_out, own.at[12]),
+    ]
+    greet(all_peers())
+    for index in vec_z + vec_x[:1]:
+        plan.start(index)
+    qkv.send_z()
+    qkv.send_x()
+    for index in trade_x:
+        plan.start(index)
+    for keep in keeps:
+        keep().start()
+    for work in (out, up, down):
+        work.send_z()
+    out.send_x()
+    for index in trade_cot:
+        plan.start(index)
+    for j in range(1, 4):
+        plan.arrived(vec_z[j - 1])
+        plan.start(vec_x[j])
+    for j in range(1, 4):
+        qkv.task_z(j)
+    up.send_x()
+    down.send_x()
+    for j in range(4):
+        qkv.task_x(j)
+    for index in vec_x:
+        plan.arrived(index)
+    for keep in keeps[:3]:
+        keep().wait()
+    for index in trade_x:
+        plan.arrived(index)
+    qkv.end()
+    for put in puts[:3]:
+        put().start()
+
+    tile = 256
+    rows = share * LEN
+    spread = [vec_all[t, 0:16, :].astype(F32) for t in range(8)]
+    vectors = spread[0]
+    for t in range(1, 8):
+        vectors = vectors + spread[t]
+    for part in range(3):
+        for col in range(0, D, tile):
+            at = part * D + col
+            weight = w_all[:, :, at : at + tile].reshape(D, tile)
+            value = jnp.dot(x_all[...].reshape(rows, D), weight, preferred_element_type=F32)
+            if part != 1:
+                value = value + vectors[part // 2 : part // 2 + 1, col : col + tile]
+            acts[:, at : at + tile] = value.astype(BF16)
+    puts[3]().start()
+
+    tasks = {
+        0: [lambda j=j: out.task_z(j) for j in (1, 2, 3)],
+        1: [lambda j=j: out.task_x(j) for j in range(4)],
+        2: [lambda: up.task_z(1)],
+        3: [lambda: up.task_z(2), lambda: up.task_z(3)],
+        4: [lambda: up.task_x(0), lambda: up.task_x(1)],
+        5: [lambda: up.task_x(2), lambda: up.task_x(3)],
+        6: [lambda: up.task_y(0), lambda: up.task_y(1)],
+        7: [lambda: up.task_y(2), lambda: down.task_z(1)],
+        8: [lambda: up.task_y(3), lambda: down.task_x(0)],
+        9: [lambda: up.task_y(4), lambda: down.task_z(2)],
+        10: [lambda: up.task_y(5), lambda: down.task_x(1)],
+        11: [lambda: up.task_y(6), lambda: down.task_z(3)],
+        12: [lambda: down.task_x(2), lambda: down.task_x(3)],
+    }
+
+    def step(s, carry):
+        for when, todo in tasks.items():
+            if when < STEPS:
+
+                @pl.when(s == when)
+                def _(todo=todo):
+                    for task in todo:
+                        task()
+
+        t, h = s // (STEPS // share), s % (STEPS // share)
+        base = pl.multiple_of(t * LEN, LEN)
+        cols = [pl.ds(pl.multiple_of(part * D + h * PAIR, PAIR), PAIR) for part in range(3)]
+        attend(len_ref[t], acts, mixed, logs, t, h, base, cols)
+        return carry
+
+    lax.fori_loop(0, STEPS, step, 0)
+    for put in puts[4:]:
+        put().start()
+    for task in tasks[STEPS]:
+        task()
+    for index in trade_cot:
+        plan.arrived(index)
+    for work in (out, up, down):
+        work.end()
+    plan.finish()
+    for keep in keeps[3:]:
+        keep().wait()
+    for put in puts:
+        put().wait()
+
+
+def attend(live, acts, mixed_ref, logs_ref, t, h, base, cols):
+    masks = head_masks(BF16)
+    keys = acts[pl.ds(base, LEN), cols[1]]
+    values = acts[pl.ds(base, LEN), cols[2]]
+    rows = 256
+    key_at = lax.broadcasted_iota(jnp.int32, (1, LEN), 1)
+    bias = jnp.where(key_at < live, 0.0, NEGATIVE)
+    lane = lax.broadcasted_iota(jnp.int32, (1, PAIR), 1)
+    for start in range(0, LEN, rows):
+        query = acts[pl.ds(base + start, rows), cols[0]] * jnp.asarray(HD ** (-0.5), BF16)
+        mixed, logs = [], []
+        for head in range(2):
+            scores = back_mul(query * masks[head], keys) + bias
+            top = jnp.max(scores, axis=-1, keepdims=True)
+            raised = jnp.exp(scores - top)
+            total = jnp.sum(raised, axis=-1, keepdims=True)
+            probs = (raised * (1.0 / total)).astype(BF16)
+            mixed.append(jnp.dot(probs, values, preferred_element_type=F32))
+            logs.append(top + jnp.log(total))
+        mixed_ref[pl.ds(base + start, rows), cols[0]] = jnp.where(
+            lane < HD, mixed[0], mixed[1]
+        ).astype(BF16)
+        flat = jnp.where(lane < HD, logs[0], logs[1]).T
+        logs_ref[t, h, 0:1, start : start + rows] = flat[0:1, :]
+        logs_ref[t, h, 1:2, start : start + rows] = flat[HD : HD + 1, :]
+
+
+def gather_all(lengths, tables, cotangent, qkv, out, up, down, vec):
     share, span = tables.shape[0] // 4, tables.shape[1] * 4
     vmem = pl.BlockSpec(memory_space=pltpu.VMEM)
     hbm = pl.BlockSpec(memory_space=pl.ANY)
     shape = lambda a: jax.ShapeDtypeStruct((8,) + a.shape[1:], BF16)
+    rows = share * span
+    logs = (share, STEPS // share, 8, LEN)
     return pl.pallas_call(
         gather_kernel,
-        in_specs=[vmem] * 7,
-        out_specs=[hbm] * 7,
+        in_specs=[pl.BlockSpec(memory_space=pltpu.SMEM)] + [vmem] * 7,
+        out_specs=[hbm] * 10,
         out_shape=[
             jax.ShapeDtypeStruct((share, span, D), BF16),
             jax.ShapeDtypeStruct((share, span, D), BF16),
-            shape(up), shape(down), shape(qkv), shape(out), shape(vec),
+            shape(qkv), shape(out), shape(up), shape(down), shape(vec),
+            jax.ShapeDtypeStruct((rows, 3 * D), BF16),
+            jax.ShapeDtypeStruct((rows, D), BF16),
+            jax.ShapeDtypeStruct(logs, F32),
         ],
         scratch_shapes=[
-            pltpu.SemaphoreType.DMA((N_WIRES,)),
-            pltpu.SemaphoreType.DMA((N_WIRES,)),
-            pltpu.SemaphoreType.DMA((7,)),
+            pltpu.VMEM((share, span, D), BF16),
+            pltpu.VMEM((8,) + qkv.shape[1:], BF16),
+            pltpu.VMEM((8,) + vec.shape[1:], BF16),
+            pltpu.VMEM((rows, 3 * D), BF16),
+            pltpu.VMEM((rows, D), BF16),
+            pltpu.VMEM(logs, F32),
+            pltpu.SemaphoreType.DMA((G_WIRES,)),
+            pltpu.SemaphoreType.DMA((G_WIRES,)),
+            pltpu.SemaphoreType.DMA((13,)),
         ],
         compiler_params=pltpu.CompilerParams(
             collective_id=0, has_side_effects=True, vmem_limit_bytes=VMEM_ALL
         ),
-        name="gather_all",
-    )(tables, cotangent, up, down, qkv, out, vec)
+        name="gather_attend",
+    )(lengths, tables, cotangent, qkv, out, up, down, vec)
 
 
 class Plan:
@@ -664,27 +790,31 @@
     table_count, local_len = tables.shape[:2]
     share = table_count // blocks
     tuned = shards == 8 and blocks == 4
-    vec_pad = jnp.pad(vectors.astype(BF16).T, ((0, 4), (0, 128 - vectors.shape[0])))
-    narrow = [w.astype(BF16) for w in (w_up, w_down, w_qkv, w_out)]
+    owned = vectors.shape[0]
+    vec_own = jnp.pad(vectors.astype(BF16).T, ((0, 4), (0, 0)))
+    narrow = [w.astype(BF16) for w in (w_qkv, w_out, w_up, w_down)]
+    my_lengths = lax.dynamic_slice(lengths, (lax.axis_index("blk") * share,), (share,))
     if tuned:
-        mine, cot, *wholes = gather_all(
-            tables, cotangent, *[w[None] for w in narrow], vec_pad[None]
+        at_own = (0, lax.axis_index("tab") * owned)
+        vec_wide = lax.dynamic_update_slice(jnp.zeros((16, D), BF16), vec_own, at_own)
+        mine, cot, *wholes, qkv, mixed, logs = gather_all(
+            my_lengths, tables, cotangent, *[w[None] for w in narrow], vec_wide[None]
         )
+        vec_f = jnp.sum(wholes[4].astype(F32), axis=0)[:12]
     else:
         spread = partial(lax.all_to_all, axis_name="blk", split_axis=0, concat_axis=1, tiled=True)
         mine, cot = spread(tables), spread(cotangent)
-        wholes = [lax.all_gather(w, "tab", axis=0) for w in narrow + [vec_pad]]
-    full_up, full_down, full_qkv, full_out = [
+        wholes = [lax.all_gather(w, "tab", axis=0) for w in narrow + [vec_own]]
+        vec_f = wholes[4][:, :12].transpose(1, 0, 2).reshape(12, D).astype(F32)
+    full_qkv, full_out, full_up, full_down = [
         w.reshape(-1, w.shape[-1]) for w in wholes[:4]
     ]
-    vec_f = wholes[4][:, :12, : vectors.shape[0]].transpose(1, 0, 2).reshape(12, D).astype(F32)
-    my_lengths = lax.dynamic_slice(lengths, (lax.axis_index("blk") * share,), (share,))
     bias_up = vec_f[8:12].reshape(-1)
-    bias_qkv = jnp.concatenate([vec_f[0], jnp.zeros((D,), F32), vec_f[1]])
-
     rows = mine.reshape(-1, D)
-    qkv = (jnp.dot(rows, full_qkv, preferred_element_type=F32) + bias_qkv).astype(BF16)
-    mixed, logs = attention_forward(my_lengths, qkv, share)
+    if not tuned:
+        bias_qkv = jnp.concatenate([vec_f[0], jnp.zeros((D,), F32), vec_f[1]])
+        qkv = (jnp.dot(rows, full_qkv, preferred_element_type=F32) + bias_qkv).astype(BF16)
+        mixed, logs = attention_forward(my_lengths, qkv, share)
     attn_out = jnp.dot(mixed, full_out, preferred_element_type=F32) + vec_f[2]
     normed_one, norm_one_back = jax.vjp(
         layer_norm, rows.astype(F32) + attn_out, vec_f[4], vec_f[5]
@@ -724,7 +854,6 @@
             grad_b1.reshape(4, D),
         ]
     )
-    owned = vectors.shape[0]
     if tuned:
         pads = ((0, 0), (0, 0), (0, 2), (0, 128 - owned))
         wide_vec = jnp.pad(gw_vec.reshape(2, 6, shards, owned).transpose(2, 0, 1, 3), pads)

time: 448 us -> 413 us (0.922)
  Pallas kernels: 301 us -> 272 us
  matrix products: 92.8 us -> 86 us
    pallas_call x2 -> x1, Pallas kernels: 141 us -> 99.4 us  [gather_all(): pl.pallas_call(gather_kernel, in_specs=[pl.BlockSpec(memory_space=pltpu.S...]
    pallas_call x1, Pallas kernels: 134 us -> 148 us  [reduce_all(): pl.pallas_call(reduce_kernel, in_specs=[vmem] * 2 + [hbm] * 5, out_specs=...]
    dot_general x1 -> x0, matrix products: 8.47 us -> none  [local(): jnp.dot(rows, full_qkv, preferred_element_type=F32) + bias_qkv]
where the time goes in v3:
time: 413 us; the launch traced here: 405 us
  Pallas kernels  272 us (66%)
  matrix products  86 us (21%)
  other arithmetic  32.6 us (8%)
  local copies, waits for them, and re-layouts  11.3 us (3%)
    pallas_call x1, Pallas kernels, reduce_all(): pl.pallas_call(reduce_kernel, in_specs=[vmem] * 2 + [hbm] * 5, out_specs=...  148 us
    pallas_call x1, Pallas kernels, gather_all(): pl.pallas_call(gather_kernel, in_specs=[pl.BlockSpec(memory_space=pltpu.S...  99.4 us
    dot_general x4, matrix products, inner(): lax.dot_general(left, right, (((0,), (0,)), ((), ())), preferred_element_...  31.5 us
    dot_general x4, matrix products, back_mul(): lax.dot_general(left, right, (((1,), (1,)), ((), ())), preferred_element_...  30.5 us
    pallas_call x1, Pallas kernels, attention_backward(): pl.pallas_call(attn_bwd_kernel, grid_spec=pltpu.PrefetchScalarGridSpec(nu...  25.3 us
    dot_general x1, matrix products, local(): hidden = jnp.dot(normed_b, full_up, preferred_element_type=F32) + bias_up  14.9 us
    convert_element_type x5, other arithmetic, adam(): return (moment_new, square_new, master_new, master_new.astype(BF16))  11.6 us

profile of v3, /device:TPU:0, one launch (start us, length us, event | category | flops | bytes accessed | tf_op | source)
XLA Modules:
  0.0 404.6 jit_solution(13142994409890946095)
XLA Ops:
  1.5 1.2 dynamic_slice.3.len_ref
  3.7 1.6 convert_bitcast_fusion.3.out_in
  5.3 2.0 convert_bitcast_fusion.2.qkv_in
  7.3 2.2 convert_bitcast_fusion.1.up_in
  10.3 99.4 %gather_attend.1 = (bf16[2,512,768]{2,1,0:T(8,128)(2,1)}, bf16[2,512,768]{2,1,0:T(8,128)(2,1)}, bf16[8,96,2304]{2,1,0:T(8,128)(2,1)}, bf16[8,96,768]{2,1,0:T(8,1...) custom-call(s32[2]{0:T(128)} %dynamic_slice.3.len_ref, ...), custom_call_target="tpu_custom_call" | custom-call | tf_op jit(solution)/shard_map/gather_attend/pallas_call | solution.py:464
  109.7 1.0 convert_reduce_fusion.1
  110.6 1.7 convert_reduce_fusion
  112.4 3.8 fusion.50
  116.7 14.9 %fusion.4 = (bf16[1024,3072]{1,0:T(8,128)(2,1)}, bf16[1024,3072]{1,0:T(8,128)(2,1)S(1)}) fusion(f32[3072]{0:T(1024)S(1)} %add.186, bf16[768,3072]{1,0:T(8,128)(2,1)} %bitcast.81, f32[1024,768]{1,0:T(8,128)S(1)} %get-tuple-element.108, f32[768]{0:T(1024)S(1)} %get-tuple-element.71, f32[768]{0:T(1024)S(1)} %get-tuple-element.72, f32[1024]{0:T(1024)S(1)} %fusion.23, ...), kind=kOutput, calls=%fused_computation.5 | convolution fusion | flops 4873519104 | bytes 20473856 | tf_op jit(solution)/shard_map/dot_general | solution.py:823
  131.7 5.4 %fusion.51 = (f32[1024]{0:T(1024)S(1)}, f32[1024,768]{1,0:T(8,128)S(1)}) fusion(f32[768]{0:T(1024)S(1)} %get-tuple-element.70, bf16[1024,3072]{1,0:T(8,128)(2,1)S(1)} %get-tuple-element.49, bf16[3072,768]{1,0:T(8,128)(2,1)S(1)} %bitcast.85, f32[768]{0:T(1024)S(1)} %get-tuple-element.71, f32[768]{0:T(1024)S(1)} %get-tuple-element.72, f32[1024]{0:T(1024)S(1)} %fusion.23, ...), kind=kOutput, calls=%fused_computation.108 | convolution fusion | flops 4837342208 | bytes 17323008 | tf_op jit(solution)/shard_map/dot_general | solution.py:828
  138.5 1.3 fusion.10
  139.8 2.6 fusion.49
  142.4 7.4 %convolution_convert_fusion = bf16[3072,768]{1,0:T(8,128)(2,1)} fusion(bf16[1024,3072]{1,0:T(8,128)(2,1)S(1)} %get-tuple-element.49, f32[1024,768]{1,0:T(8,128)S(1)} %get-tuple-element.98, f32[1024]{0:T(1024)S(1)} %negate_multiply_fusion.1), kind=kOutput, calls=%fused_computation.11 | convolution fusion | flops 4835770368 | bytes 14159872 | tf_op jit(solution)/shard_map/dot_general | solution.py:40
  150.1 10.0 %fusion.5 = (f32[3072]{0:T(1024)S(1)}, f32[1024,3072]{1,0:T(8,128)}) fusion(bf16[1024,3072]{1,0:T(8,128)(2,1)} %get-tuple-element.51, bf16[3072,768]{1,0:T(8,128)(2,1)S(1)} %bitcast.86, f32[1024,768]{1,0:T(8,128)S(1)} %get-tuple-element.98, f32[1024]{0:T(1024)S(1)} %negate_multiply_fusion.1), kind=kOutput, calls=%fused_computation.9 | convolution fusion | flops 4842845184 | bytes 26755072 | tf_op jit(solution)/shard_map/dot_general | solution.py:44
  160.1 12.6 %multiply_reduce_fusion = (f32[768]{0:T(1024)S(1)}, f32[1024]{0:T(1024)S(1)}, f32[768]{0:T(1024)S(1)}, f32[1024,768]{1,0:T(8,128)}) fusion(f32[1024,768]{1,0:T(8,128)S(1)} %get-tuple-element.108, f32[1024]{0:T(1024)S(1)} %fusion.23, f32[1024]{0:T(1024)S(1)} %broadcast_multiply_fusion.1, f32[768]{0:T(1024)S(1)} %get-tuple-element.72, ...), kind=kOutput, calls=%fused_computation.24 | convolution fusion | flops 4849136640 | bytes 33055744 | tf_op jit(solution)/shard_map/dot_general | solution.py:44
  172.7 14.0 %convolution_convert_fusion.1 = bf16[768,3072]{1,0:T(8,128)(2,1)} fusion(f32[1024,3072]{1,0:T(8,128)} %get-tuple-element.113, bf16[1024,3072]{1,0:T(8,128)(2,1)} %get-tuple-element.51, f32[1024,768]{1,0:T(8,128)S(1)} %get-tuple-element.108, f32[768]{0:T(1024)S(1)} %get-tuple-element.71, f32[768]{0:T(1024)S(1)} %get-tuple-element.72, f32[1024]{0:T(1024)S(1)} %fusion.23, ...), kind=kOutput, calls=%fused_computation.12 | convolution fusion | flops 4847566848 | bytes 26753024 | tf_op jit(solution)/shard_map/dot_general | solution.py:40
  186.7 2.8 fusion.48
  189.8 1.3 copy-done.1
  191.7 2.6 convolution_convert_fusion.3.do_ref
  194.3 25.3 %attn_bwd.1 = (bf16[3,1024,768]{2,1,0:T(8,128)(2,1)}, f32[2,6,8,128]{3,2,1,0:T(8,128)}) custom-call(s32[2]{0:T(128)} %dynamic_slice.3.len_ref, bf16[1024,2304]{1,0:T(8,128)(2,1)} %get-tuple-element.52.q_ref.k_ref.v_ref, bf16[1024,2304]{1,0:T(8,128)(2,1)} %get-tuple-element.52.q_ref.k_ref.v_ref, bf16[1024,2304]{1,0:T(8,128)(2,1)} %get-tuple-element.52.q_ref.k_ref.v_ref, ...), custom_call_target="tpu_custom_call" | custom-call | tf_op jit(solution)/shard_map/attn_bwd/pallas_call | solution.py:154
  219.6 4.1 %convolution_convert_fusion.4 = bf16[768,768]{1,0:T(8,128)(2,1)} fusion(bf16[1024,768]{1,0:T(8,128)(2,1)} %get-tuple-element.46.o_ref, f32[1024,768]{1,0:T(8,128)S(1)} %copy-done.2, f32[1024]{0:T(1024)S(1)} %negate_multiply_fusion), kind=kOutput, calls=%fused_computation.46 | convolution fusion | flops 1210122240 | bytes 5902336 | tf_op jit(solution)/shard_map/dot_general | solution.py:40
  224.1 1.7 copy-done.22
  225.8 5.2 %add_convert_fusion.1 = bf16[1024,768]{1,0:T(8,128)(2,1)} fusion(f32[1024,768]{1,0:T(8,128)S(1)} %copy-done.2, f32[1024]{0:T(1024)S(1)} %negate_multiply_fusion, bf16[768,2304]{1,0:T(8,128)(2,1)S(1)} %bitcast.87, bf16[1024,768]{1,0:T(8,128)(2,1)S(1)} %get-tuple-element.102, bf16[1024,768]{1,0:T(8,128)(2,1)S(1)} %get-tuple-element.103, ...), kind=kOutput, calls=%fused_computation.26 | convolution fusion | flops 3640393728 | bytes 12980224 | tf_op jit(solution)/shard_map/dot_general | solution.py:44
  231.0 6.0 %convolution_convert_fusion.2 = bf16[768,2304]{1,0:T(8,128)(2,1)} fusion(bf16[1024,768]{1,0:T(8,128)(2,1)S(1)} %bitcast.89, bf16[1024,768]{1,0:T(8,128)(2,1)S(1)} %get-tuple-element.102, bf16[1024,768]{1,0:T(8,128)(2,1)S(1)} %get-tuple-element.103, bf16[1024,768]{1,0:T(8,128)(2,1)S(1)} %get-tuple-element.101), kind=kOutput, calls=%fused_computation.13 | convolution fusion | flops 3639803904 | bytes 9830400 | tf_op jit(solution)/shard_map/dot_general | solution.py:40
  238.7 147.7 %reduce_all.1 = (bf16[8,128,768]{2,1,0:T(8,128)(2,1)}, bf16[8,128,768]{2,1,0:T(8,128)(2,1)}, bf16[96,3072]{1,0:T(8,128)(2,1)}, bf16[384,768]{1,0:T(8,128)(2,1)},...) custom-call(bf16[2,512,768]{2,1,0:T(8,128)(2,1)} %bitcast.76, ...), custom_call_target="tpu_custom_call" | custom-call | tf_op jit(solution)/shard_map/reduce_all/pallas_call | solution.py:766
  387.7 2.1 fusion.42
  389.9 3.7 fusion.45
  393.6 1.9 convert_element_type.134
  396.9 2.5 fusion.39
  399.4 0.9 copy-done.13
  400.5 2.6 fusion.36
  403.0 1.1 copy.48
  (88 shorter events, 9.6 us)
Async XLA Ops:
  0.7 8.8 %copy-start.4 = (f32[384,768]{1,0:T(8,128)S(1)}, f32[384,768]{1,0:T(8,128)}, u32[]{:S(2)}) copy-start(f32[384,768]{1,0:T(8,128)} %param.26) | copy-start | bytes 3538948
  3.6 6.7 %copy-start.18 = (bf16[1,16,768]{2,1,0:T(8,128)(2,1)}, bf16[1,16,768]{2,1,0:T(8,128)(2,1)S(1)}, u32[]{:S(2)}) copy-start(bf16[1,16,768]{2,1,0:T(8,128)(2,1)S(1)} %dynamic_update_slice.4.vec_in) | copy-start | bytes 73732
  116.2 15.4 %slice-start = ((s8[4718592]{0:T(1024)(128)(4,1)}), s8[4194304]{0:T(1024)(128)(4,1)S(1)}, s32[]{:S(2)}) async-start(s8[4718592]{0:T(1024)(128)(4,1)} %bitcast.83), calls=%async_computation | async-start | bytes 8388608
  116.7 14.9 %slice-start.1 = ((s8[4718592]{0:T(1024)(128)(4,1)}), s8[524288]{0:T(1024)(128)(4,1)S(1)}, s32[]{:S(2)}) async-start(s8[4718592]{0:T(1024)(128)(4,1)} %bitcast.83), calls=%async_computation.1 | async-start | bytes 1048576
  137.1 1.4 copy-start
  189.5 1.7 copy-start.1
  189.5 2.1 copy-start.24
  194.3 25.3 %copy-start.2 = (f32[1024,768]{1,0:T(8,128)S(1)}, f32[1024,768]{1,0:T(8,128)}, u32[]{:S(2)}) copy-start(f32[1024,768]{1,0:T(8,128)} %copy-done.1) | copy-start | bytes 9437188
  219.6 4.1 %copy-start.6 = (bf16[3,1024,768]{2,1,0:T(8,128)(2,1)S(1)}, bf16[3,1024,768]{2,1,0:T(8,128)(2,1)}, u32[]{:S(2)}) copy-start(bf16[3,1024,768]{2,1,0:T(8,128)(2,1)} %get-tuple-element.54) | copy-start | bytes 14155780
  223.8 2.0 copy-start.22
  225.8 5.2 %copy-start.23 = (bf16[2,512,768]{2,1,0:T(8,128)(2,1)S(1)}, bf16[2,512,768]{2,1,0:T(8,128)(2,1)}, u32[]{:S(2)}) copy-start(bf16[2,512,768]{2,1,0:T(8,128)(2,1)} %get-tuple-element.45) | copy-start | bytes 4718596
  238.6 148.5 %copy-start.19 = (f32[96,12]{0,1:T(8,128)S(1)}, f32[96,12]{0,1:T(8,128)}, u32[]{:S(2)}) copy-start(f32[96,12]{0,1:T(8,128)} %param.27) | copy-start | bytes 13828
  238.6 148.5 %copy-start.20 = (f32[96,12]{0,1:T(8,128)S(1)}, f32[96,12]{0,1:T(8,128)}, u32[]{:S(2)}) copy-start(f32[96,12]{0,1:T(8,128)} %param.37) | copy-start | bytes 13828
  238.6 148.5 %copy-start.21 = (f32[96,12]{0,1:T(8,128)S(1)}, f32[96,12]{0,1:T(8,128)}, u32[]{:S(2)}) copy-start(f32[96,12]{0,1:T(8,128)} %param.32) | copy-start | bytes 13828
  238.6 149.1 %copy-start.14 = (f32[96,768]{1,0:T(8,128)S(1)}, f32[96,768]{1,0:T(8,128)}, u32[]{:S(2)}) copy-start(f32[96,768]{1,0:T(8,128)} %param.24) | copy-start | bytes 884740
  238.6 149.1 %copy-start.17 = (f32[96,768]{1,0:T(8,128)S(1)}, f32[96,768]{1,0:T(8,128)}, u32[]{:S(2)}) copy-start(f32[96,768]{1,0:T(8,128)} %param.34) | copy-start | bytes 884740
  238.6 151.2 %copy-start.7 = (f32[96,2304]{1,0:T(8,128)S(1)}, f32[96,2304]{1,0:T(8,128)}, u32[]{:S(2)}) copy-start(f32[96,2304]{1,0:T(8,128)} %param.23) | copy-start | bytes 2654212
  389.9 3.7 copy-start.9
  393.6 2.0 copy-start.3
  393.6 2.6 copy-start.10
  393.6 3.1 copy-start.11
  393.6 3.3 copy-start.16
  396.8 2.6 copy-start.5
  396.8 2.6 copy-start.12
  396.8 3.5 copy-start.13
  396.8 3.6 copy-start.15
  400.5 2.6 copy-start.8
